TPU v7x, 32 devices: a whole 2x2x4 slice. The times are simulated.
32 devices in a mesh: section: 4 (over z), tensor: 4 (over y, core), dp: 2 (over x).
Axes of the slice: x: 2, y: 2, z: 4, core: 2. Of those that a mesh axis runs over, the one named last changes fastest.
Arguments:
- hidden: bfloat16 [4096, 5120], P(('dp', 'section'), 'tensor'), parts along dimension 0, may hold values from -6 to 6
- queries: bfloat16 [4096, 2560], P(('dp', 'section'), 'tensor'), parts along dimension 0, may hold values from -6 to 6
- key_vectors: bfloat16 [4096, 2560], P(('dp', 'section'), 'tensor'), parts along dimension 0, may hold values from -6 to 6
- value_vectors: bfloat16 [4096, 2560], P(('dp', 'section'), 'tensor'), parts along dimension 0, may hold values from -6 to 6
- gate_logits: float32 [4096, 20], P(('dp', 'section'), 'tensor'), parts along dimension 0, may hold values from -6 to 6
- decay_index: int32 [20], P('tensor'), may hold values from 5 to 15
- norm_gain: float32 [2560], P('tensor'), may hold values from 0.25 to 1.75
- out_weight: bfloat16 [2560, 5120], P('tensor'), may hold values from -0.125 to 0.125
Outputs:
- layer_output: bfloat16 [4096, 5120], P(('dp', 'section'), 'tensor'), parts along dimension 0
There are 2 independent parts, one for each index of `dp`. A program takes and returns all parts, laid end to end along the dimension named above; an argument that names none is the same for every part. Nothing has to cross between parts.
All inputs are finite; a program needn't handle non-finite values.
Results may differ from a plain program's by a relative error of at most 0.0055.
The roundings to bfloat16 on the way count: a program that leaves them out, or rounds other values in their place, can miss the bound.
Values sent between devices are 32-bit elements; how exact they have to be, the bound alone decides.
No kernel may reach another device: no remote copies, remote signals or barrier semaphores. Data moves between devices by JAX's collectives and lax.ppermute only.
A program may use at most 64 MiB of HBM per device.

v0:
```python
import functools

import numpy as np

import jax
import jax.numpy as jnp
from jax import lax
from jax.experimental import pallas as pl
from jax.experimental.pallas import tpu as pltpu
from jax.sharding import PartitionSpec as P


HD = 128
HALF = HD // 2
EPSILON = 1e-05
LANES = 128
F32 = jnp.float32
BF16 = jnp.bfloat16


VMEM_SPEC = pl.BlockSpec(memory_space=pltpu.VMEM)
SMEM_SPEC = pl.BlockSpec(memory_space=pltpu.SMEM)
ANY_SPEC = pl.BlockSpec(memory_space=pl.ANY)


def angle_tables(row_count, n_section):
    frequency = 10000.0 ** (-(np.arange(HALF, dtype=np.float64) * 2.0 / HD))
    frequency = np.concatenate([frequency, frequency])
    near = np.arange(row_count, dtype=np.float64)[:, None] * frequency[None, :]
    far = (np.arange(n_section, dtype=np.float64) * row_count)[:, None] * frequency[None, :]
    return tuple(f(x).astype(np.float32) for x in (near, far) for f in (np.cos, np.sin))


def rotation(index_ref, near_cos, near_sin, far_cos, far_sin):
    section = index_ref[0]
    cos_far = far_cos[pl.ds(section, 1), :]
    sin_far = far_sin[pl.ds(section, 1), :]
    lane = lax.broadcasted_iota(jnp.int32, (1, HD), 1)
    sign = jnp.where(lane < HALF, -1.0, 1.0)
    cosine = near_cos[...] * cos_far - near_sin[...] * sin_far
    sine = near_cos[...] * (sin_far * sign) + near_sin[...] * (cos_far * sign)
    return cosine, sine


def rotate(x, cosine, sine):
    x = x.astype(F32)
    return x * cosine + pltpu.roll(x, HALF, 1) * sine


def state_kernel(heads, groups, index_ref, decay_ref, gates_ref, k_ref, v_ref, nc, ns, fc, fs, *outs):
    state_refs = outs[: len(groups)]
    total_refs = outs[len(groups) : 2 * len(groups)]
    row_ref, column_ref, grown_ref = outs[2 * len(groups) :]
    rows = k_ref.shape[0]
    blocks = rows // LANES
    gates = gates_ref[...]
    if heads < 8:
        gates = jnp.concatenate([gates, jnp.zeros((8 - heads, rows), F32)], axis=0)
    head_row = lax.broadcasted_iota(jnp.int32, (8, LANES), 0)
    exponent = jnp.zeros((8, LANES), F32)
    for h in range(heads):
        exponent = jnp.where(head_row == h, decay_ref[h].astype(F32), exponent)
    rate = jnp.exp2(-exponent)[:, :1]
    soft = jnp.maximum(gates, 0.0) + jnp.log1p(jnp.exp(-jnp.abs(gates)))
    log_decay = -rate * soft
    stacked = jnp.concatenate(
        [log_decay[:, b * LANES : (b + 1) * LANES] for b in range(blocks)], axis=0
    )
    high = stacked.astype(BF16)
    rest = stacked - high.astype(F32)
    middle = rest.astype(BF16)
    low = (rest - middle.astype(F32)).astype(BF16)
    parts = jnp.concatenate([high, middle, low], axis=0)
    upper = (
        lax.broadcasted_iota(jnp.int32, (LANES, LANES), 0)
        <= lax.broadcasted_iota(jnp.int32, (LANES, LANES), 1)
    )
    sums = jnp.dot(
        parts, jnp.where(upper, 1.0, 0.0).astype(BF16), preferred_element_type=F32
    )
    span = 8 * blocks
    sums = sums[:span] + sums[span : 2 * span] + sums[2 * span :]
    offset = jnp.zeros((8, 1), F32)
    pieces = []
    for b in range(blocks):
        piece = sums[8 * b : 8 * b + 8] + offset
        pieces.append(piece)
        offset = piece[:, LANES - 1 :]
    row_ref[...] = jnp.concatenate(pieces, axis=1)
    totals = jnp.broadcast_to(jnp.exp(offset), (8, LANES))
    flat = jnp.concatenate(pieces, axis=0)
    ends = jnp.concatenate([offset] * blocks, axis=0)
    pad = jnp.zeros((LANES - span, LANES), F32)
    column = jnp.concatenate([flat, pad], axis=0).T
    grown = jnp.concatenate([jnp.exp(flat), pad], axis=0).T
    fading = jnp.concatenate([jnp.exp(ends - flat), pad], axis=0).T
    for b in range(blocks):
        column_ref[b * LANES : (b + 1) * LANES, :] = column[:, 8 * b : 8 * b + 8]
        grown_ref[b * LANES : (b + 1) * LANES, :] = grown[:, 8 * b : 8 * b + 8]
    cosine, sine = rotation(index_ref, nc, ns, fc, fs)
    cosine = cosine * HD ** (-0.5)
    sine = sine * HD ** (-0.5)
    first = 0
    for state_ref, total_ref, width in zip(state_refs, total_refs, groups):
        for i in range(width):
            h = first + i
            total_ref[i] = totals[h : h + 1]
            cols = slice(h * HD, (h + 1) * HD)
            rot_k = rotate(k_ref[:, cols], cosine, sine).astype(BF16).astype(F32)
            fade = jnp.concatenate(
                [
                    jnp.broadcast_to(fading[:, 8 * b + h : 8 * b + h + 1], (LANES, HD))
                    for b in range(blocks)
                ],
                axis=0,
            )
            weighted = (rot_k * fade).astype(BF16)
            state_ref[i] = lax.dot_general(
                weighted, v_ref[:, cols], (((0,), (0,)), ((), ())), preferred_element_type=F32
            )
        first += width


def intra_kernel(heads, index_ref, q_ref, k_ref, v_ref, row_ref, column_ref, nc, ns, fc, fs, intra_ref, rot_ref):
    rows = q_ref.shape[0]
    block = min(256, rows)
    cosine, sine = rotation(index_ref, nc, ns, fc, fs)
    causal = lax.broadcasted_iota(jnp.int32, (block, block), 0) >= lax.broadcasted_iota(
        jnp.int32, (block, block), 1
    )
    for h in range(heads):
        cols = slice(h * HD, (h + 1) * HD)
        rot_q = rotate(q_ref[:, cols], cosine, sine).astype(BF16)
        rot_k = (rotate(k_ref[:, cols], cosine, sine) * HD ** (-0.5)).astype(BF16)
        rot_ref[:, cols] = rot_q
        for t in range(rows // block):
            own = slice(t * block, (t + 1) * block)
            here = jnp.broadcast_to(column_ref[own, h : h + 1], (block, block))
            total = jnp.zeros((block, HD), F32)
            for s in range(t + 1):
                other = slice(s * block, (s + 1) * block)
                score = lax.dot_general(
                    rot_q[own], rot_k[other], (((1,), (1,)), ((), ())), preferred_element_type=F32
                )
                gap = here - row_ref[h : h + 1, other]
                if s == t:
                    gap = jnp.where(causal, gap, -1e30)
                kept = (score * jnp.exp(gap)).astype(BF16)
                total = total + jnp.dot(kept, v_ref[other, cols], preferred_element_type=F32)
            intra_ref[own, cols] = total


def finish_kernel(heads, groups, received, low, high, index_ref, block_ref, intra_ref, rot_ref, grown_ref, gain_ref, weight_ref, *rest):
    states = received * len(groups)
    state_refs = rest[:states]
    earlier_refs = rest[states:-4]
    kept_ref, part_ref, weight_vmem, sem = rest[-4:]
    width = weight_vmem.shape[1]
    copy = pltpu.make_async_copy(
        weight_ref.at[:, pl.ds(pl.multiple_of(block_ref[0] * width, LANES), width)], weight_vmem, sem
    )
    copy.start()
    chosen = index_ref[0]
    first = 0
    for g, count in enumerate(groups):
        for i in range(count):
            h = first + i
            cols = slice(h * HD, (h + 1) * HD)
            state = jnp.zeros((HD, HD), F32)
            for r in range(received):
                state = jnp.where(chosen == r + 1, state_refs[r * len(groups) + g][i], state)
            carried = jnp.dot(rot_ref[low:high, cols], state.astype(BF16), preferred_element_type=F32)
            combined = intra_ref[low:high, cols] + jnp.broadcast_to(
                grown_ref[low:high, h : h + 1], (high - low, HD)
            ) * carried
            average = jnp.mean(combined, axis=-1, keepdims=True)
            centered = combined - average
            variance = jnp.mean(centered * centered, axis=-1, keepdims=True)
            gain = gain_ref[cols].reshape(1, HD)
            normed = centered * lax.rsqrt(variance + EPSILON) * gain
            kept_ref[kept_ref.shape[0] - (high - low) :, cols] = normed.astype(BF16)
        first += count
    if earlier_refs:
        kept_ref[:low, :] = earlier_refs[0][...]
    copy.wait()
    part_ref[...] = jnp.dot(
        kept_ref[kept_ref.shape[0] - (high - low) :, :], weight_vmem[...], preferred_element_type=F32
    )


def finish(groups, chosen, block, intra, rot_q, grown, gain, weight, received, earlier, low, high, columns):
    width = rot_q.shape[1]
    flat = [piece for stage in received for piece in stage]
    earlier = [] if earlier is None else [earlier]
    size = high if earlier else high - low
    return pl.pallas_call(
        functools.partial(finish_kernel, sum(groups), groups, len(received), low, high),
        in_specs=[SMEM_SPEC] * 2 + [VMEM_SPEC] * 4 + [ANY_SPEC] + [VMEM_SPEC] * len(flat + earlier),
        out_specs=[VMEM_SPEC] * 2,
        out_shape=[
            jax.ShapeDtypeStruct((size, width), BF16),
            jax.ShapeDtypeStruct((high - low, columns), F32),
        ],
        scratch_shapes=[pltpu.VMEM((width, columns), BF16), pltpu.SemaphoreType.DMA],
        cost_estimate=pl.CostEstimate(
            flops=2 * (high - low) * width * columns,
            bytes_accessed=2 * width * columns + 4 * (high - low) * (columns + 2 * width),
            transcendentals=0,
        ),
    )(chosen, block, intra, rot_q, grown, gain, weight, *flat, *earlier)


def project_kernel(cuts, extras, block_ref, kept_ref, weight_ref, *rest):
    low, high = cuts[0], cuts[-1]
    total = jnp.dot(kept_ref[low:high, :], weight_ref[...], preferred_element_type=F32)
    for extra in rest[:extras]:
        total = total + extra[...].astype(F32)
    for out_ref, a, b in zip(rest[extras:], cuts[:-1], cuts[1:]):
        out_ref[...] = total[a - low : b - low]


def project(kept, weight, block, cuts, columns, extras=(), tile=640):
    depth = weight.shape[0]
    tile = min(tile, columns)
    steps = columns // tile
    rows = cuts[-1] - cuts[0]
    spans = [b - a for a, b in zip(cuts[:-1], cuts[1:])]
    return pl.pallas_call(
        functools.partial(project_kernel, cuts, len(extras)),
        grid_spec=pltpu.PrefetchScalarGridSpec(
            num_scalar_prefetch=1,
            grid=(steps,),
            in_specs=[
                pl.BlockSpec((cuts[-1], depth), lambda j, b: (0, 0)),
                pl.BlockSpec((depth, tile), lambda j, b: (0, b[0] * steps + j)),
            ]
            + [pl.BlockSpec((rows, tile), lambda j, b: (0, j)) for _ in extras],
            out_specs=[pl.BlockSpec((n, tile), lambda j, b: (0, j)) for n in spans],
        ),
        out_shape=[jax.ShapeDtypeStruct((n, columns), F32) for n in spans],
        cost_estimate=pl.CostEstimate(
            flops=2 * rows * depth * columns,
            bytes_accessed=2 * depth * columns + 4 * rows * columns * (1 + len(extras)),
            transcendentals=0,
        ),
    )(block, kept, weight, *extras)


def pass_states(states, totals, n_section, n_dp, section):
    if n_section == 4:
        outer, inner = {0: 1, 1: 0, 2: 3, 3: 2}, {1: 2, 2: 1}
        received = [[] for _ in range(3)]
        for state, decay in zip(states, totals):
            sent = state
            for stage, partner in enumerate((outer, inner, outer)):
                if stage:
                    sent = state + decay * received[stage - 1][-1]
                pairs = [
                    (z * n_dp + d, partner[z] * n_dp + d if z in partner else z * n_dp + (d ^ 1) % n_dp)
                    for z in range(n_section)
                    for d in range(n_dp)
                ]
                received[stage].append(lax.ppermute(sent, ("section", "dp"), pairs))
        return received, section
    own = jnp.concatenate(states, axis=0)
    decays = lax.all_gather(jnp.concatenate(totals, axis=0)[:, 0, 0], "section", axis=0)
    gathered = lax.all_gather(own, "section", axis=0)

    def advance(carry, piece):
        decay, state = piece
        return decay[:, None, None] * carry + state, carry

    _, entering = lax.scan(advance, jnp.zeros_like(own), (decays, gathered))
    mine = lax.dynamic_index_in_dim(entering, section, 0, keepdims=False)
    parts, first = [], 0
    for state in states:
        parts.append(mine[first : first + state.shape[0]])
        first += state.shape[0]
    return [parts], jnp.int32(1)


def local(n_section, n_tensor, n_dp, hidden, queries, key_vectors, value_vectors, gate_logits, decay_index, norm_gain, out_weight):
    rows, width = queries.shape
    heads = decay_index.shape[0]
    columns = hidden.shape[1]
    groups = [heads - heads // 2, heads // 2]
    section = lax.axis_index("section").astype(jnp.int32)
    me = lax.axis_index("tensor").astype(jnp.int32)
    tables = angle_tables(rows, n_section)
    place = section.reshape(1)

    outs = pl.pallas_call(
        functools.partial(state_kernel, heads, groups),
        in_specs=[SMEM_SPEC] * 2 + [VMEM_SPEC] * 7,
        out_specs=[VMEM_SPEC] * (2 * len(groups) + 3),
        out_shape=[jax.ShapeDtypeStruct((g, HD, HD), F32) for g in groups]
        + [jax.ShapeDtypeStruct((g, 1, LANES), F32) for g in groups]
        + [
            jax.ShapeDtypeStruct((8, rows), F32),
            jax.ShapeDtypeStruct((rows, 8), F32),
            jax.ShapeDtypeStruct((rows, 8), F32),
        ],
    )(place, decay_index.astype(jnp.int32), gate_logits.T, key_vectors, value_vectors, *tables)
    states = outs[: len(groups)]
    totals = outs[len(groups) : 2 * len(groups)]
    decay_row, decay_column, grown = outs[2 * len(groups) :]

    received, chosen = pass_states(states, totals, n_section, n_dp, section)

    intra, rot_q = pl.pallas_call(
        functools.partial(intra_kernel, heads),
        in_specs=[SMEM_SPEC] + [VMEM_SPEC] * 9,
        out_specs=[VMEM_SPEC] * 2,
        out_shape=[
            jax.ShapeDtypeStruct((rows, width), F32),
            jax.ShapeDtypeStruct((rows, width), BF16),
        ],
        cost_estimate=pl.CostEstimate(
            flops=4 * rows * rows * width, bytes_accessed=12 * rows * width, transcendentals=rows * rows * heads
        ),
    )(place, queries, key_vectors, value_vectors, decay_row, decay_column, *tables)

    def block_of(bit):
        return (me ^ bit).reshape(1) if n_tensor == 4 else jnp.zeros((1,), jnp.int32)

    start = rows * 3 // 8
    common = (groups, chosen.reshape(1), block_of(3), intra, rot_q, grown, norm_gain, out_weight, received)
    kept, part = finish(*common, None, 0, start, columns)

    if n_tensor != 4:
        kept, _ = finish(*common, kept, start, rows, columns)
        product = lax.dot_general(kept, out_weight, (((1,), (0,)), ((), ())), preferred_element_type=F32)
        summed = lax.psum_scatter(product, "tensor", scatter_dimension=1, tiled=True)
        return (hidden.astype(F32) + summed).astype(BF16)

    def swap(x, bit):
        return lax.ppermute(x, "tensor", [(i, i ^ bit) for i in range(n_tensor)])

    cuts = [start, rows * 5 // 8, rows * 7 // 8, rows]
    part = swap(part, 1)
    (lead,) = project(kept, out_weight, block_of(2), [0, start], columns)
    lead = lead + part
    arrived = [swap(lead, 2)]
    kept, rest = finish(*common, kept, start, rows, columns)
    rest = swap(rest, 1)
    (near,) = project(kept, out_weight, block_of(1), [0, rows], columns)
    near = swap(near, 1)
    crossing = project(kept, out_weight, block_of(2), cuts, columns, (rest,))
    for piece in crossing:
        arrived.append(swap(piece, 2))
    (own,) = project(kept, out_weight, block_of(0), [0, rows], columns, (hidden, near))
    result = None
    for low, far in zip([0] + cuts, arrived):
        high = low + far.shape[0]
        piece = (own[low:high] + far).astype(BF16)
        if result is None:
            result = jnp.pad(piece, ((0, rows - high), (0, 0)))
        else:
            result = lax.dynamic_update_slice(result, piece, (low, 0))
    return result


def solution(mesh):
    rows = P(("dp", "section"), "tensor")
    placed = (rows, rows, rows, rows, rows, P("tensor"), P("tensor"), P("tensor", None))

    def body(*arrays):
        return local(*(mesh.shape[n] for n in ("section", "tensor", "dp")), *arrays)

    return jax.shard_map(body, mesh=mesh, in_specs=placed, out_specs=rows, check_vma=False)
```

profile of v0, /device:TPU:0, one launch (start us, length us, event | category | flops | bytes accessed | tf_op | source)
XLA Modules:
  0.0 116.6 jit_solution(12188535494413601158)
XLA Ops:
  0.0 3.8 %shard_map.118 = (f32[3,128,128]{2,1,0:T(8,128)}, f32[2,128,128]{2,1,0:T(8,128)}, f32[3,1,128]{2,1,0:T(1,128)}, f32[2,1,128]{2,1,0:T(1,128)}, f32[8,512]{1,0:T(8...) custom-call(s32[1]{0:T(128)} %bitcast.1.index_ref, s32[5]{0:T(128)} %decay_ref.1, f32[5,512]{1,0:T(8,128)} %bitcast.12, ...), custom_call_target="tpu_custom_call" | custom-call | tf_op jit(solution)/shard_map/pallas_call | solution.py:292
  3.8 3.1 %collective-permute-start = (f32[3,128,128]{2,1,0:T(8,128)}, f32[3,128,128]{2,1,0:T(8,128)S(1)}, u32[]{:S(2)}, u32[]{:S(2)}) collective-permute-start(f32[3,128,128]{2,1,0:T(8,128)} %get-tuple-element.26), channel_id=1, source_target_pairs={{0,8},{1,9},{8,0},{9,1},{16,24},{17,25},{24,16},{25,17},{2,10},{3,... | collective-permute-start | bytes 589832 | tf_op jit(solution)/shard_map/ppermute | solution.py:263
  6.9 0.1 collective-permute-start.1
  7.0 0.7 copy.15
  7.7 5.2 %collective-permute-done.rest_0_ = f32[3,128,128]{2,1,0:T(8,128)S(1)} collective-permute-done((f32[3,128,128]{2,1,0:T(8,128)}, f32[3,128,128]{2,1,0:T(8,128)S(1)}, u32[]{:S(2)}, u32[]{:S(2)}) %collective-permute-start) | collective-permute-done | bytes 196640 | tf_op jit(solution)/shard_map/ppermute | solution.py:263
  12.9 1.0 multiply_add_fusion.1
  13.9 2.0 %collective-permute-start.2 = (f32[3,128,128]{2,1,0:T(8,128)S(1)}, f32[3,128,128]{2,1,0:T(8,128)S(1)}, u32[]{:S(2)}, u32[]{:S(2)}) collective-permute-start(f32[3,128,128]{2,1,0:T(8,128)S(1)} %multiply_add_fusion.1), channel_id=1, source_target_pairs={{0,1},{1,0},{8,16},{9,17},{16,8},{17,9},{24,25},{25,24},{2,3},{3,2... | collective-permute-start | bytes 589832 | tf_op jit(solution)/shard_map/ppermute | solution.py:263
  15.9 0.0 collective-permute-done.1.rest_1_
  15.9 1.0 multiply_add_fusion.3
  16.9 0.6 collective-permute-start.3
  17.5 3.5 %collective-permute-done.2.rest_2_ = f32[3,128,128]{2,1,0:T(8,128)S(1)} collective-permute-done((f32[3,128,128]{2,1,0:T(8,128)S(1)}, f32[3,128,128]{2,1,0:T(8,128)S(1)}, u32[]{:S(2)}, u32[]{:S(2)}) %collective-permute-start.2) | collective-permute-done | bytes 196640 | tf_op jit(solution)/shard_map/ppermute | solution.py:263
  21.1 1.0 multiply_add_fusion
  22.1 1.7 %collective-permute-start.4 = (f32[3,128,128]{2,1,0:T(8,128)S(1)}, f32[3,128,128]{2,1,0:T(8,128)S(1)}, u32[]{:S(2)}, u32[]{:S(2)}) collective-permute-start(f32[3,128,128]{2,1,0:T(8,128)S(1)} %multiply_add_fusion), channel_id=1, source_target_pairs={{0,8},{1,9},{8,0},{9,1},{16,24},{17,25},{24,16},{25,17},{2,10},{3,... | collective-permute-start | bytes 589832 | tf_op jit(solution)/shard_map/ppermute | solution.py:263
  23.8 0.0 collective-permute-done.3.rest_3_
  23.8 0.4 collective-permute-start.5
  24.3 5.0 %shard_map.119 = (f32[512,640]{1,0:T(8,128)}, bf16[512,640]{1,0:T(8,128)(2,1)}) custom-call(s32[1]{0:T(128)} %bitcast.1.index_ref, bf16[512,640]{1,0:T(8,128)(2,1)} %q_ref.1, bf16[512,640]{1,0:T(8,128)(2,1)} %k_ref.3, bf16[512,640]{1,0:T(8,128)(2,1)} %v_ref.3, f32[8,512]{1,0:T(8,128)} %get-tuple-element.21.row_ref, f32[512,8]{1,0:T(8,128)} %get-tuple-element.22.column_ref, ...), custom_call_target="tpu_custom_call" | custom-call | flops 671088640 | bytes 3932160 | tf_op jit(solution)/shard_map/pallas_call | solution.py:310
  29.3 0.0 collective-permute-done.5.rest_5_
  29.3 0.0 collective-permute-done.4.rest_4_
  29.3 0.6 copy-done.8
  29.9 0.1 copy-done.7
  30.0 4.8 %shard_map.120 = (bf16[192,640]{1,0:T(8,128)(2,1)}, f32[192,1280]{1,0:T(8,128)}) custom-call(s32[1]{0:T(128)} %bitcast.1.index_ref, s32[1]{0:T(128)} %bitcast.2.block_ref, f32[512,640]{1,0:T(8,128)} %get-tuple-element.23.intra_ref, bf16[512,640]{1,0:T(8,128)(2,1)} %get-tuple-element.24.rot_ref, f32[512,8]{1,0:T(8,128)} %get-tuple-element.25.grown_ref, ...), custom_call_target="tpu_custom_call" | custom-call | flops 314572800 | bytes 3604480 | tf_op jit(solution)/shard_map/pallas_call | solution.py:196
  34.9 5.4 %shard_map.121 = (bf16[512,640]{1,0:T(8,128)(2,1)}, f32[320,1280]{1,0:T(8,128)}) custom-call(s32[1]{0:T(128)} %bitcast.1.index_ref, s32[1]{0:T(128)} %bitcast.2.block_ref, f32[512,640]{1,0:T(8,128)} %get-tuple-element.23.intra_ref, bf16[512,640]{1,0:T(8,128)(2,1)} %get-tuple-element.24.rot_ref, f32[512,8]{1,0:T(8,128)} %get-tuple-element.25.grown_ref, ...), custom_call_target="tpu_custom_call" | custom-call | flops 524288000 | bytes 4915200 | tf_op jit(solution)/shard_map/pallas_call | solution.py:196
  40.3 4.0 %shard_map.122 = f32[512,1280]{1,0:T(8,128)} custom-call(s32[1]{0:T(128)} %bitcast.5.block_ref, bf16[512,640]{1,0:T(8,128)(2,1)} %get-tuple-element.31.kept_ref, bf16[640,5120]{1,0:T(8,128)(2,1)} %weight_ref.11), custom_call_target="tpu_custom_call" | custom-call | flops 838860800 | bytes 4259840 | tf_op jit(solution)/shard_map/pallas_call | solution.py:228
  44.3 0.0 collective-permute-start.6
  44.3 0.5 collective-permute-start.7
  44.8 2.8 %shard_map.124 = f32[192,1280]{1,0:T(8,128)} custom-call(s32[1]{0:T(128)} %bitcast.6.block_ref, bf16[192,640]{1,0:T(8,128)(2,1)} %get-tuple-element.30.rest_6_.kept_ref, bf16[640,5120]{1,0:T(8,128)(2,1)} %weight_ref.11), custom_call_target="tpu_custom_call" | custom-call | flops 314572800 | bytes 2621440 | tf_op jit(solution)/shard_map/pallas_call | solution.py:228
  47.6 3.4 %collective-permute-done.7 = f32[192,1280]{1,0:T(8,128)} collective-permute-done((f32[192,1280]{1,0:T(8,128)}, f32[192,1280]{1,0:T(8,128)}, u32[]{:S(2)}, u32[]{:S(2)}) %collective-permute-start.7) | collective-permute-done | bytes 983072 | tf_op jit(solution)/shard_map/ppermute | solution.py:337
  50.9 2.5 %add.33 = f32[192,1280]{1,0:T(8,128)} add(f32[192,1280]{1,0:T(8,128)} %shard_map.124, f32[192,1280]{1,0:T(8,128)} %collective-permute-done.7) | non-fusion elementwise | flops 245760 | bytes 2949120 | tf_op jit(solution)/shard_map/add | solution.py:342
  53.5 1.6 %collective-permute-start.8 = (f32[192,1280]{1,0:T(8,128)}, f32[192,1280]{1,0:T(8,128)}, u32[]{:S(2)}, u32[]{:S(2)}) collective-permute-start(f32[192,1280]{1,0:T(8,128)} %add.33), channel_id=1, source_target_pairs={{0,4},{2,6},{4,0},{6,2},{1,5},{3,7},{5,1},{7,3},{8,12},{10,14},{12... | collective-permute-start | bytes 2949128 | tf_op jit(solution)/shard_map/ppermute | solution.py:337
  55.1 0.0 collective-permute-done.9.rest_0_
  55.1 3.6 %shard_map.125 = (f32[128,1280]{1,0:T(8,128)}, f32[128,1280]{1,0:T(8,128)}, f32[64,1280]{1,0:T(8,128)}) custom-call(s32[1]{0:T(128)} %bitcast.6.block_ref, bf16[512,640]{1,0:T(8,128)(2,1)} %get-tuple-element.31.kept_ref, bf16[640,5120]{1,0:T(8,128)(2,1)} %weight_ref.11, f32[320,1280]{1,0:T(8,128)} %collective-permute-done.9.rest_0_), custom_call_target="tpu_custom_call" | custom-call | flops 524288000 | bytes 4915200 | tf_op jit(solution)/shard_map/pallas_call | solution.py:228
  58.7 0.4 collective-permute-start.10
  59.1 1.6 %collective-permute-start.12 = (f32[64,1280]{1,0:T(8,128)}, f32[64,1280]{1,0:T(8,128)}, u32[]{:S(2)}, u32[]{:S(2)}) collective-permute-start(f32[64,1280]{1,0:T(8,128)} %get-tuple-element.36), channel_id=1, source_target_pairs={{0,4},{2,6},{4,0},{6,2},{1,5},{3,7},{5,1},{7,3},{8,12},{10,14},{12... | collective-permute-start | bytes 983048 | tf_op jit(solution)/shard_map/ppermute | solution.py:337
  60.7 0.4 collective-permute-start.11
  61.2 0.0 collective-permute-done.6.rest_1_
  61.2 1.5 %copy-done.1 = f32[512,1280]{1,0:T(8,128)} copy-done((f32[512,1280]{1,0:T(8,128)}, f32[512,1280]{1,0:T(8,128)S(1)}, u32[]{:S(2)}) %copy-start.1) | copy-done | bytes 2621464
  62.7 4.8 %shard_map.123 = f32[512,1280]{1,0:T(8,128)} custom-call(s32[1]{0:T(128)} %bitcast.block_ref, bf16[512,640]{1,0:T(8,128)(2,1)} %get-tuple-element.31.kept_ref, bf16[640,5120]{1,0:T(8,128)(2,1)} %weight_ref.11, bf16[512,1280]{1,0:T(8,128)(2,1)} %rest_0_.1, f32[512,1280]{1,0:T(8,128)} %copy-done.1), custom_call_target="tpu_custom_call" | custom-call | flops 838860800 | bytes 9502720 | tf_op jit(solution)/shard_map/pallas_call | solution.py:228
  67.5 10.9 %collective-permute-done.8 = f32[192,1280]{1,0:T(8,128)} collective-permute-done((f32[192,1280]{1,0:T(8,128)}, f32[192,1280]{1,0:T(8,128)}, u32[]{:S(2)}, u32[]{:S(2)}) %collective-permute-start.8) | collective-permute-done | bytes 983072 | tf_op jit(solution)/shard_map/ppermute | solution.py:337
  78.4 1.7 %fusion = bf16[192,1280]{1,0:T(8,128)(2,1)S(1)} fusion(f32[192,1280]{1,0:T(8,128)} %collective-permute-done.8, f32[512,1280]{1,0:T(8,128)} %shard_map.123), kind=kLoop, calls=%fused_computation.1 | loop fusion | flops 491520 | bytes 2457600 | tf_op jit(solution)/shard_map/convert_element_type | solution.py:355
  80.2 0.1 pad.4
  80.3 12.1 %collective-permute-done.10 = f32[128,1280]{1,0:T(8,128)S(1)} collective-permute-done((f32[128,1280]{1,0:T(8,128)}, f32[128,1280]{1,0:T(8,128)S(1)}, u32[]{:S(2)}, u32[]{:S(2)}) %collective-permute-start.10) | collective-permute-done | bytes 655392 | tf_op jit(solution)/shard_map/ppermute | solution.py:337
  92.4 0.1 fusion.3
  92.4 20.3 %collective-permute-done.11 = f32[128,1280]{1,0:T(8,128)} collective-permute-done((f32[128,1280]{1,0:T(8,128)}, f32[128,1280]{1,0:T(8,128)}, u32[]{:S(2)}, u32[]{:S(2)}) %collective-permute-start.11) | collective-permute-done | bytes 655392 | tf_op jit(solution)/shard_map/ppermute | solution.py:337
  112.7 1.1 fusion.4
  113.9 0.0 copy-start.4
  113.9 0.0 collective-permute-done.12
  113.9 1.0 copy-done.4
  114.9 1.7 %fusion.6 = bf16[512,1280]{1,0:T(8,128)(2,1)} fusion(bf16[512,1280]{1,0:T(8,128)(2,1)} %copy-done.4, f32[64,1280]{1,0:T(8,128)} %collective-permute-done.12, f32[512,1280]{1,0:T(8,128)S(1)} %copy-done), kind=kLoop, calls=%fused_computation.12 | loop fusion | flops 163840 | bytes 819200 | tf_op jit(solution)/shard_map/dynamic_update_slice | solution.py:359
  (19 shorter events, 0.1 us)
Async XLA Ops:
  3.8 20.0 %copy-start.9 = (f32[2,128,128]{2,1,0:T(8,128)S(1)}, f32[2,128,128]{2,1,0:T(8,128)}, u32[]{:S(2)}) copy-start(f32[2,128,128]{2,1,0:T(8,128)} %get-tuple-element.27) | copy-start | bytes 393220
  3.8 20.0 %copy-start.10 = (f32[2,1,128]{2,1,0:T(1,128)S(1)}, f32[2,1,128]{2,1,0:T(1,128)}, u32[]{:S(2)}) copy-start(f32[2,1,128]{2,1,0:T(1,128)} %get-tuple-element.29) | copy-start | bytes 3076
  3.8 9.1 %collective-permute-start = (f32[3,128,128]{2,1,0:T(8,128)}, f32[3,128,128]{2,1,0:T(8,128)S(1)}, u32[]{:S(2)}, u32[]{:S(2)}) collective-permute-start(f32[3,128,128]{2,1,0:T(8,128)} %get-tuple-element.26), channel_id=1, source_target_pairs={{0,8},{1,9},{8,0},{9,1},{16,24},{17,25},{24,16},{25,17},{2,10},{3,... | collective-permute-start | bytes 589832 | tf_op jit(solution)/shard_map/ppermute | solution.py:263
  6.9 9.0 %collective-permute-start.1 = (f32[2,128,128]{2,1,0:T(8,128)}, f32[2,128,128]{2,1,0:T(8,128)S(1)}, u32[]{:S(2)}, u32[]{:S(2)}) collective-permute-start(f32[2,128,128]{2,1,0:T(8,128)} %get-tuple-element.27), channel_id=1, source_target_pairs={{0,8},{1,9},{8,0},{9,1},{16,24},{17,25},{24,16},{25,17},{2,10},{3,... | collective-permute-start | bytes 393224 | tf_op jit(solution)/shard_map/ppermute | solution.py:263
  12.9 16.4 %copy-start.2 = (f32[3,128,128]{2,1,0:T(8,128)}, f32[3,128,128]{2,1,0:T(8,128)S(1)}, u32[]{:S(2)}) copy-start(f32[3,128,128]{2,1,0:T(8,128)S(1)} %collective-permute-done.rest_0_) | copy-start | bytes 589828
  13.9 7.1 %collective-permute-start.2 = (f32[3,128,128]{2,1,0:T(8,128)S(1)}, f32[3,128,128]{2,1,0:T(8,128)S(1)}, u32[]{:S(2)}, u32[]{:S(2)}) collective-permute-start(f32[3,128,128]{2,1,0:T(8,128)S(1)} %multiply_add_fusion.1), channel_id=1, source_target_pairs={{0,1},{1,0},{8,16},{9,17},{16,8},{17,9},{24,25},{25,24},{2,3},{3,2... | collective-permute-start | bytes 589832 | tf_op jit(solution)/shard_map/ppermute | solution.py:263
  15.9 13.3 %copy-start.5 = (f32[2,128,128]{2,1,0:T(8,128)}, f32[2,128,128]{2,1,0:T(8,128)S(1)}, u32[]{:S(2)}) copy-start(f32[2,128,128]{2,1,0:T(8,128)S(1)} %collective-permute-done.1.rest_1_) | copy-start | bytes 393220
  16.9 6.9 %collective-permute-start.3 = (f32[2,128,128]{2,1,0:T(8,128)S(1)}, f32[2,128,128]{2,1,0:T(8,128)S(1)}, u32[]{:S(2)}, u32[]{:S(2)}) collective-permute-start(f32[2,128,128]{2,1,0:T(8,128)S(1)} %multiply_add_fusion.3), channel_id=1, source_target_pairs={{0,1},{1,0},{8,16},{9,17},{16,8},{17,9},{24,25},{25,24},{2,3},{3,2... | collective-permute-start | bytes 393224 | tf_op jit(solution)/shard_map/ppermute | solution.py:263
  21.1 8.2 %copy-start.3 = (f32[3,128,128]{2,1,0:T(8,128)}, f32[3,128,128]{2,1,0:T(8,128)S(1)}, u32[]{:S(2)}) copy-start(f32[3,128,128]{2,1,0:T(8,128)S(1)} %collective-permute-done.2.rest_2_) | copy-start | bytes 589828
  22.1 7.2 %collective-permute-start.4 = (f32[3,128,128]{2,1,0:T(8,128)S(1)}, f32[3,128,128]{2,1,0:T(8,128)S(1)}, u32[]{:S(2)}, u32[]{:S(2)}) collective-permute-start(f32[3,128,128]{2,1,0:T(8,128)S(1)} %multiply_add_fusion), channel_id=1, source_target_pairs={{0,8},{1,9},{8,0},{9,1},{16,24},{17,25},{24,16},{25,17},{2,10},{3,... | collective-permute-start | bytes 589832 | tf_op jit(solution)/shard_map/ppermute | solution.py:263
  23.8 5.5 %copy-start.6 = (f32[2,128,128]{2,1,0:T(8,128)}, f32[2,128,128]{2,1,0:T(8,128)S(1)}, u32[]{:S(2)}) copy-start(f32[2,128,128]{2,1,0:T(8,128)S(1)} %collective-permute-done.3.rest_3_) | copy-start | bytes 393220
  23.8 5.4 %collective-permute-start.5 = (f32[2,128,128]{2,1,0:T(8,128)S(1)}, f32[2,128,128]{2,1,0:T(8,128)S(1)}, u32[]{:S(2)}, u32[]{:S(2)}) collective-permute-start(f32[2,128,128]{2,1,0:T(8,128)S(1)} %multiply_add_fusion.2), channel_id=1, source_target_pairs={{0,8},{1,9},{8,0},{9,1},{16,24},{17,25},{24,16},{25,17},{2,10},{3,... | collective-permute-start | bytes 393224 | tf_op jit(solution)/shard_map/ppermute | solution.py:263
  29.3 0.7 copy-start.8
  29.3 0.7 copy-start.7
  44.3 16.9 %collective-permute-start.6 = (f32[512,1280]{1,0:T(8,128)}, f32[512,1280]{1,0:T(8,128)S(1)}, u32[]{:S(2)}, u32[]{:S(2)}) collective-permute-start(f32[512,1280]{1,0:T(8,128)} %shard_map.122), channel_id=1, source_target_pairs={{0,2},{2,0},{4,6},{6,4},{1,3},{3,1},{5,7},{7,5},{8,10},{10,8},{12,... | collective-permute-start | bytes 7864328 | tf_op jit(solution)/shard_map/ppermute | solution.py:337
  44.3 6.7 %collective-permute-start.7 = (f32[192,1280]{1,0:T(8,128)}, f32[192,1280]{1,0:T(8,128)}, u32[]{:S(2)}, u32[]{:S(2)}) collective-permute-start(f32[192,1280]{1,0:T(8,128)} %get-tuple-element.32), channel_id=1, source_target_pairs={{0,2},{2,0},{4,6},{6,4},{1,3},{3,1},{5,7},{7,5},{8,10},{10,8},{12,... | collective-permute-start | bytes 2949128 | tf_op jit(solution)/shard_map/ppermute | solution.py:337
  44.8 10.3 %collective-permute-start.9 = (f32[320,1280]{1,0:T(8,128)}, f32[320,1280]{1,0:T(8,128)}, u32[]{:S(2)}, u32[]{:S(2)}) collective-permute-start(f32[320,1280]{1,0:T(8,128)} %get-tuple-element.33), channel_id=1, source_target_pairs={{0,2},{2,0},{4,6},{6,4},{1,3},{3,1},{5,7},{7,5},{8,10},{10,8},{12,... | collective-permute-start | bytes 4915208 | tf_op jit(solution)/shard_map/ppermute | solution.py:337
  53.5 24.9 %collective-permute-start.8 = (f32[192,1280]{1,0:T(8,128)}, f32[192,1280]{1,0:T(8,128)}, u32[]{:S(2)}, u32[]{:S(2)}) collective-permute-start(f32[192,1280]{1,0:T(8,128)} %add.33), channel_id=1, source_target_pairs={{0,4},{2,6},{4,0},{6,2},{1,5},{3,7},{5,1},{7,3},{8,12},{10,14},{12... | collective-permute-start | bytes 2949128 | tf_op jit(solution)/shard_map/ppermute | solution.py:337
  58.7 33.7 %collective-permute-start.10 = (f32[128,1280]{1,0:T(8,128)}, f32[128,1280]{1,0:T(8,128)S(1)}, u32[]{:S(2)}, u32[]{:S(2)}) collective-permute-start(f32[128,1280]{1,0:T(8,128)} %get-tuple-element.34), channel_id=1, source_target_pairs={{0,4},{2,6},{4,0},{6,2},{1,5},{3,7},{5,1},{7,3},{8,12},{10,14},{12... | collective-permute-start | bytes 1966088 | tf_op jit(solution)/shard_map/ppermute | solution.py:337
  59.1 54.7 %collective-permute-start.12 = (f32[64,1280]{1,0:T(8,128)}, f32[64,1280]{1,0:T(8,128)}, u32[]{:S(2)}, u32[]{:S(2)}) collective-permute-start(f32[64,1280]{1,0:T(8,128)} %get-tuple-element.36), channel_id=1, source_target_pairs={{0,4},{2,6},{4,0},{6,2},{1,5},{3,7},{5,1},{7,3},{8,12},{10,14},{12... | collective-permute-start | bytes 983048 | tf_op jit(solution)/shard_map/ppermute | solution.py:337
  60.7 52.0 %collective-permute-start.11 = (f32[128,1280]{1,0:T(8,128)}, f32[128,1280]{1,0:T(8,128)}, u32[]{:S(2)}, u32[]{:S(2)}) collective-permute-start(f32[128,1280]{1,0:T(8,128)} %get-tuple-element.35), channel_id=1, source_target_pairs={{0,4},{2,6},{4,0},{6,2},{1,5},{3,7},{5,1},{7,3},{8,12},{10,14},{12... | collective-permute-start | bytes 1966088 | tf_op jit(solution)/shard_map/ppermute | solution.py:337
  61.2 1.6 %copy-start.1 = (f32[512,1280]{1,0:T(8,128)}, f32[512,1280]{1,0:T(8,128)S(1)}, u32[]{:S(2)}) copy-start(f32[512,1280]{1,0:T(8,128)S(1)} %collective-permute-done.6.rest_1_) | copy-start | bytes 7864324
  78.4 13.9 %copy-start = (f32[512,1280]{1,0:T(8,128)S(1)}, f32[512,1280]{1,0:T(8,128)}, u32[]{:S(2)}) copy-start(f32[512,1280]{1,0:T(8,128)} %shard_map.123) | copy-start | bytes 7864324
  113.9 1.1 copy-start.4
where the time goes:
time: 117 us
  waiting for transfers between devices  55.4 us (47%)
  Pallas kernels  34.2 us (29%)
  starting transfers between devices  12.6 us (11%)
  other arithmetic  10.2 us (9%)
  local copies, waits for them, and re-layouts  4.09 us (3%)
    ppermute x7, waiting for transfers between devices, swap(): return lax.ppermute(x, 'tensor', [(i, i ^ bit) for i in range(n_tensor)])  46.7 us
    pallas_call x4, Pallas kernels, project(): pl.pallas_call(functools.partial(project_kernel, cuts, len(extras)), grid...  15.2 us
    pallas_call x2, Pallas kernels, finish(): pl.pallas_call(functools.partial(finish_kernel, sum(groups), groups, len(...  10.2 us
    ppermute x6, waiting for transfers between devices, pass_states(): received[stage].append(lax.ppermute(sent, ('section', 'dp'), pairs))  8.74 us
    ppermute x6, starting transfers between devices, pass_states(): received[stage].append(lax.ppermute(sent, ('section', 'dp'), pairs))  8 us
    pallas_call x1, Pallas kernels, local(): pl.pallas_call(functools.partial(intra_kernel, heads), in_specs=[SMEM_SPE...  4.96 us
    ppermute x7, starting transfers between devices, swap(): return lax.ppermute(x, 'tensor', [(i, i ^ bit) for i in range(n_tensor)])  4.56 us
    unnamed x23, local copies, waits for them, and re-layouts  4 us
  transfers between devices with their start and end apart: 13, of which 6 were waited for; matrix products, arithmetic and copies ran while one was open for 8% of the time, Pallas kernels for 14%

commit v1 on v0

--- a/solution.py
+++ b/solution.py
@@ -150,16 +150,52 @@
             intra_ref[own, cols] = total
 
 
-def finish_kernel(heads, groups, received, low, high, index_ref, block_ref, intra_ref, rot_ref, grown_ref, gain_ref, weight_ref, *rest):
-    states = received * len(groups)
-    state_refs = rest[:states]
-    earlier_refs = rest[states:-4]
-    kept_ref, part_ref, weight_vmem, sem = rest[-4:]
-    width = weight_vmem.shape[1]
-    copy = pltpu.make_async_copy(
-        weight_ref.at[:, pl.ds(pl.multiple_of(block_ref[0] * width, LANES), width)], weight_vmem, sem
-    )
-    copy.start()
+def spread_kernel(row_ref, block_ref, other_ref, same_in, other_in, *outs):
+    half = outs[0].shape[0]
+    for i, source in enumerate((same_in, other_in)):
+        for j in range(2):
+            outs[2 * i + j][...] = source[j * half : (j + 1) * half, :].astype(F32)
+
+
+def spread(weight, quarter, same, other, columns):
+    rows = weight.shape[0] // 4
+    return pl.pallas_call(
+        spread_kernel,
+        grid_spec=pltpu.PrefetchScalarGridSpec(
+            num_scalar_prefetch=3,
+            grid=(1,),
+            in_specs=[
+                pl.BlockSpec((rows, columns), lambda i, q, s, o: (q[0], s[0])),
+                pl.BlockSpec((rows, columns), lambda i, q, s, o: (q[0], o[0])),
+            ],
+            out_specs=[pl.BlockSpec((rows // 2, columns), lambda i, q, s, o: (0, 0))] * 4,
+        ),
+        out_shape=[jax.ShapeDtypeStruct((rows // 2, columns), F32)] * 4,
+    )(quarter, same, other, weight, weight)
+
+
+def widen_kernel(block_ref, weight_ref, out_ref):
+    out_ref[...] = weight_ref[...].astype(F32)
+
+
+def widen(weight, block, columns, tile=128):
+    depth = weight.shape[0]
+    return pl.pallas_call(
+        widen_kernel,
+        grid_spec=pltpu.PrefetchScalarGridSpec(
+            num_scalar_prefetch=1,
+            grid=(depth // tile,),
+            in_specs=[pl.BlockSpec((tile, columns), lambda i, b: (i, b[0]))],
+            out_specs=pl.BlockSpec((tile, columns), lambda i, b: (i, 0)),
+        ),
+        out_shape=jax.ShapeDtypeStruct((depth, columns), F32),
+    )(block, weight)
+
+
+def finish_kernel(heads, groups, received, index_ref, intra_ref, rot_ref, grown_ref, gain_ref, *rest):
+    state_refs, (kept_ref, *wide_refs) = rest[: received * len(groups)], rest[received * len(groups) :]
+    rows = intra_ref.shape[0]
+    size = rows // len(wide_refs)
     chosen = index_ref[0]
     first = 0
     for g, count in enumerate(groups):
@@ -169,81 +205,122 @@
             state = jnp.zeros((HD, HD), F32)
             for r in range(received):
                 state = jnp.where(chosen == r + 1, state_refs[r * len(groups) + g][i], state)
-            carried = jnp.dot(rot_ref[low:high, cols], state.astype(BF16), preferred_element_type=F32)
-            combined = intra_ref[low:high, cols] + jnp.broadcast_to(
-                grown_ref[low:high, h : h + 1], (high - low, HD)
+            carried = jnp.dot(rot_ref[:, cols], state.astype(BF16), preferred_element_type=F32)
+            combined = intra_ref[:, cols] + jnp.broadcast_to(
+                grown_ref[:, h : h + 1], (rows, HD)
             ) * carried
             average = jnp.mean(combined, axis=-1, keepdims=True)
             centered = combined - average
             variance = jnp.mean(centered * centered, axis=-1, keepdims=True)
             gain = gain_ref[cols].reshape(1, HD)
-            normed = centered * lax.rsqrt(variance + EPSILON) * gain
-            kept_ref[kept_ref.shape[0] - (high - low) :, cols] = normed.astype(BF16)
+            normed = (centered * lax.rsqrt(variance + EPSILON) * gain).astype(BF16)
+            kept_ref[:, cols] = normed
+            for p, wide_ref in enumerate(wide_refs):
+                wide_ref[:, cols] = normed[p * size : (p + 1) * size].astype(F32)
         first += count
-    if earlier_refs:
-        kept_ref[:low, :] = earlier_refs[0][...]
-    copy.wait()
-    part_ref[...] = jnp.dot(
-        kept_ref[kept_ref.shape[0] - (high - low) :, :], weight_vmem[...], preferred_element_type=F32
-    )
-
-
-def finish(groups, chosen, block, intra, rot_q, grown, gain, weight, received, earlier, low, high, columns):
-    width = rot_q.shape[1]
+
+
+def finish(groups, chosen, intra, rot_q, grown, gain, received, parts):
+    rows, width = rot_q.shape
     flat = [piece for stage in received for piece in stage]
-    earlier = [] if earlier is None else [earlier]
-    size = high if earlier else high - low
     return pl.pallas_call(
-        functools.partial(finish_kernel, sum(groups), groups, len(received), low, high),
-        in_specs=[SMEM_SPEC] * 2 + [VMEM_SPEC] * 4 + [ANY_SPEC] + [VMEM_SPEC] * len(flat + earlier),
-        out_specs=[VMEM_SPEC] * 2,
-        out_shape=[
-            jax.ShapeDtypeStruct((size, width), BF16),
-            jax.ShapeDtypeStruct((high - low, columns), F32),
-        ],
-        scratch_shapes=[pltpu.VMEM((width, columns), BF16), pltpu.SemaphoreType.DMA],
-        cost_estimate=pl.CostEstimate(
-            flops=2 * (high - low) * width * columns,
-            bytes_accessed=2 * width * columns + 4 * (high - low) * (columns + 2 * width),
-            transcendentals=0,
-        ),
-    )(chosen, block, intra, rot_q, grown, gain, weight, *flat, *earlier)
-
-
-def project_kernel(cuts, extras, block_ref, kept_ref, weight_ref, *rest):
-    low, high = cuts[0], cuts[-1]
-    total = jnp.dot(kept_ref[low:high, :], weight_ref[...], preferred_element_type=F32)
-    for extra in rest[:extras]:
-        total = total + extra[...].astype(F32)
-    for out_ref, a, b in zip(rest[extras:], cuts[:-1], cuts[1:]):
-        out_ref[...] = total[a - low : b - low]
-
-
-def project(kept, weight, block, cuts, columns, extras=(), tile=640):
+        functools.partial(finish_kernel, sum(groups), groups, len(received)),
+        in_specs=[SMEM_SPEC] + [VMEM_SPEC] * (4 + len(flat)),
+        out_specs=[VMEM_SPEC] * (1 + parts),
+        out_shape=[jax.ShapeDtypeStruct((rows, width), BF16)]
+        + [jax.ShapeDtypeStruct((rows // parts, width), F32)] * parts,
+    )(chosen, intra, rot_q, grown, gain, *flat)
+
+
+def chip_kernel(parts, block_ref, kept_ref, weight_ref, wide_ref, hidden_ref, *rest):
+    total = jnp.dot(kept_ref[...], weight_ref[...], preferred_element_type=F32)
+    total = total + hidden_ref[...].astype(F32)
+    wide = wide_ref[...].astype(BF16)
+    size = kept_ref.shape[0] // parts
+    for p in range(parts):
+        rest[parts + p][...] = total[p * size : (p + 1) * size] + jnp.dot(
+            rest[p][...].astype(BF16), wide, preferred_element_type=F32
+        )
+
+
+def chip_sum(kept, weight, block, wide, hidden, pieces, tile=640):
     depth = weight.shape[0]
-    tile = min(tile, columns)
+    rows, columns = hidden.shape
+    parts = len(pieces)
     steps = columns // tile
-    rows = cuts[-1] - cuts[0]
-    spans = [b - a for a, b in zip(cuts[:-1], cuts[1:])]
     return pl.pallas_call(
-        functools.partial(project_kernel, cuts, len(extras)),
+        functools.partial(chip_kernel, parts),
         grid_spec=pltpu.PrefetchScalarGridSpec(
             num_scalar_prefetch=1,
             grid=(steps,),
             in_specs=[
-                pl.BlockSpec((cuts[-1], depth), lambda j, b: (0, 0)),
+                pl.BlockSpec((rows, depth), lambda j, b: (0, 0)),
                 pl.BlockSpec((depth, tile), lambda j, b: (0, b[0] * steps + j)),
+                pl.BlockSpec((depth, tile), lambda j, b: (0, j)),
+                pl.BlockSpec((rows, tile), lambda j, b: (0, j)),
             ]
-            + [pl.BlockSpec((rows, tile), lambda j, b: (0, j)) for _ in extras],
-            out_specs=[pl.BlockSpec((n, tile), lambda j, b: (0, j)) for n in spans],
+            + [pl.BlockSpec((rows // parts, depth), lambda j, b: (0, 0))] * parts,
+            out_specs=[pl.BlockSpec((rows // parts, tile), lambda j, b: (0, j))] * parts,
         ),
-        out_shape=[jax.ShapeDtypeStruct((n, columns), F32) for n in spans],
-        cost_estimate=pl.CostEstimate(
-            flops=2 * rows * depth * columns,
-            bytes_accessed=2 * depth * columns + 4 * rows * columns * (1 + len(extras)),
-            transcendentals=0,
+        out_shape=[jax.ShapeDtypeStruct((rows // parts, columns), F32)] * parts,
+    )(block, kept, weight, wide, hidden, *pieces)
+
+
+def gather_kernel(bits, n_rows, n_sources, quarter_ref, *refs):
+    totals = refs[:n_rows]
+    sources = refs[n_rows : n_rows + n_rows * n_sources]
+    pieces = refs[n_rows * (1 + n_sources) : n_rows * (1 + n_sources) + 2 * n_sources * len(bits)]
+    outs = refs[len(refs) - 1 - (len(refs) - 1 - n_rows * (1 + n_sources) - len(pieces)) : -1]
+    padded = refs[-1]
+    half = pieces[0].shape[0]
+    sums = [total[...] for total in totals]
+    slot = 0
+    for b, bit in enumerate(bits):
+        quarter = quarter_ref[0] ^ bit
+        start = pl.multiple_of(quarter * LANES, LANES)
+        skip = pl.multiple_of(quarter * (2 * half - LANES), 32)
+        for n in range(n_sources):
+            padded[slot] = jnp.zeros(padded.shape[1:], BF16)
+            for j in range(2):
+                padded[slot, pl.ds(skip + j * half, half), :] = pieces[
+                    2 * (b * n_sources + n) + j
+                ][...].astype(BF16)
+            for i in range(n_rows):
+                window = sources[i * n_sources + n][:, pl.ds(start, 2 * LANES)].astype(BF16)
+                sums[i] = sums[i] + jnp.dot(window, padded[slot], preferred_element_type=F32)
+            slot += 1
+    if len(outs) == n_rows:
+        for out, value in zip(outs, sums):
+            out[...] = value.astype(out.dtype)
+    else:
+        size = sums[0].shape[0]
+        for i, value in enumerate(sums):
+            outs[0][i * size : (i + 1) * size, :] = value.astype(outs[0].dtype)
+
+
+def gather_sum(totals, sources, pieces, bits, quarter, joined, tile=640):
+    rows, columns = totals[0].shape
+    width = sources[0][0].shape[1]
+    n_rows, n_sources = len(sources), len(sources[0])
+    half = pieces[0][0][0].shape[0]
+    flat = [x for b in pieces for n in b for x in n]
+    if joined:
+        out_shape = [jax.ShapeDtypeStruct((n_rows * rows, columns), BF16)]
+    else:
+        out_shape = [jax.ShapeDtypeStruct((rows, columns), F32)] * n_rows
+    return pl.pallas_call(
+        functools.partial(gather_kernel, bits, n_rows, n_sources),
+        grid_spec=pltpu.PrefetchScalarGridSpec(
+            num_scalar_prefetch=1,
+            grid=(columns // tile,),
+            in_specs=[pl.BlockSpec((rows, tile), lambda j, q: (0, j))] * n_rows
+            + [pl.BlockSpec((rows, width), lambda j, q: (0, 0))] * (n_rows * n_sources)
+            + [pl.BlockSpec((half, tile), lambda j, q: (0, j))] * len(flat),
+            out_specs=[pl.BlockSpec((x.shape[0], tile), lambda j, q: (0, j)) for x in out_shape],
+            scratch_shapes=[pltpu.VMEM((n_sources * len(bits), 2 * LANES, tile), BF16)],
         ),
-    )(block, kept, weight, *extras)
+        out_shape=out_shape,
+    )(quarter, *totals, *[x for row in sources for x in row], *flat)
 
 
 def pass_states(states, totals, n_section, n_dp, section):
@@ -289,6 +366,26 @@
     tables = angle_tables(rows, n_section)
     place = section.reshape(1)
 
+    gathers = n_tensor == 4 and n_dp == 2 and n_section % 2 == 0 and width == 5 * LANES
+    sizes = {"tensor": n_tensor, "section": n_section, "dp": n_dp}
+
+    def swap(x, axis, bit):
+        return lax.ppermute(x, axis, [(i, i ^ bit) for i in range(sizes[axis])])
+
+    def block_of(bit):
+        return (me ^ bit).reshape(1)
+
+    if gathers:
+        quarter = (2 * lax.axis_index("dp").astype(jnp.int32) + section % 2).reshape(1)
+        sent = spread(out_weight, quarter, block_of(2), block_of(3), columns)
+        pieces = {"y": [[swap(sent[2 * n + j], "tensor", 2 + n) for j in range(2)] for n in range(2)]}
+        pieces["x"] = [[swap(pieces["y"][n][j], "dp", 1) for j in range(2)] for n in range(2)]
+        pieces["z"] = [[swap(pieces["y"][n][j], "section", 1) for j in range(2)] for n in range(2)]
+        pieces["d"] = [
+            [swap(pieces["z"][0][j], "dp", 1) for j in range(2)],
+            [swap(pieces["x"][1][j], "section", 1) for j in range(2)],
+        ]
+
     outs = pl.pallas_call(
         functools.partial(state_kernel, heads, groups),
         in_specs=[SMEM_SPEC] * 2 + [VMEM_SPEC] * 7,
@@ -320,43 +417,25 @@
         ),
     )(place, queries, key_vectors, value_vectors, decay_row, decay_column, *tables)
 
-    def block_of(bit):
-        return (me ^ bit).reshape(1) if n_tensor == 4 else jnp.zeros((1,), jnp.int32)
-
-    start = rows * 3 // 8
-    common = (groups, chosen.reshape(1), block_of(3), intra, rot_q, grown, norm_gain, out_weight, received)
-    kept, part = finish(*common, None, 0, start, columns)
-
-    if n_tensor != 4:
-        kept, _ = finish(*common, kept, start, rows, columns)
+    parts = 2
+    kept, *wide = finish(groups, chosen.reshape(1), intra, rot_q, grown, norm_gain, received, parts)
+    if not gathers:
         product = lax.dot_general(kept, out_weight, (((1,), (0,)), ((), ())), preferred_element_type=F32)
         summed = lax.psum_scatter(product, "tensor", scatter_dimension=1, tiled=True)
         return (hidden.astype(F32) + summed).astype(BF16)
 
-    def swap(x, bit):
-        return lax.ppermute(x, "tensor", [(i, i ^ bit) for i in range(n_tensor)])
-
-    cuts = [start, rows * 5 // 8, rows * 7 // 8, rows]
-    part = swap(part, 1)
-    (lead,) = project(kept, out_weight, block_of(2), [0, start], columns)
-    lead = lead + part
-    arrived = [swap(lead, 2)]
-    kept, rest = finish(*common, kept, start, rows, columns)
-    rest = swap(rest, 1)
-    (near,) = project(kept, out_weight, block_of(1), [0, rows], columns)
-    near = swap(near, 1)
-    crossing = project(kept, out_weight, block_of(2), cuts, columns, (rest,))
-    for piece in crossing:
-        arrived.append(swap(piece, 2))
-    (own,) = project(kept, out_weight, block_of(0), [0, rows], columns, (hidden, near))
-    result = None
-    for low, far in zip([0] + cuts, arrived):
-        high = low + far.shape[0]
-        piece = (own[low:high] + far).astype(BF16)
-        if result is None:
-            result = jnp.pad(piece, ((0, rows - high), (0, 0)))
-        else:
-            result = lax.dynamic_update_slice(result, piece, (low, 0))
+    beside = widen(out_weight, block_of(1), columns)
+    beside = swap(beside, "tensor", 1)
+    far_wide = [swap(x, "tensor", 2) for x in wide]
+    chip_wide = [swap(x, "tensor", 1) for x in wide]
+    totals = chip_sum(kept, out_weight, block_of(0), beside, hidden, chip_wide)
+    across = [swap(x, "tensor", 1) for x in far_wide]
+    sources = [[x, y] for x, y in zip(far_wide, across)]
+    early, late = [pieces[k] for k in "yxz"], [pieces["d"]]
+    totals = list(totals)
+    for i in range(parts):
+        totals[i : i + 1] = gather_sum(totals[i : i + 1], sources[i : i + 1], early, (0, 2, 1), quarter, False)
+    (result,) = gather_sum(totals, sources, late, (3,), quarter, True)
     return result
 
 

time: 117 us -> 139 us (1.19)
  starting transfers between devices: 12.6 us -> 25.3 us
  waiting for transfers between devices: 55.4 us -> 66.2 us
  Pallas kernels: 34.2 us -> 41.6 us
  other arithmetic: 10.2 us -> 3.54 us
  local copies, waits for them, and re-layouts: 4.09 us -> 1.43 us
    pallas_call x4 -> x6, Pallas kernels: 15.2 us -> 28.3 us  [the longest x3 15 us: gather_sum(): pl.pallas_call(functools.partial(gather_kernel, bits, n_rows, n_sources),...]
    ppermute x6, waiting for transfers between devices: 8.74 us -> 21.7 us  [pass_states(): received[stage].append(lax.ppermute(sent, ('section', 'dp'), pairs))]
    ppermute x7 -> x23, starting transfers between devices: 4.56 us -> 16.6 us  [swap(): return lax.ppermute(x, axis, [(i, i ^ bit) for i in range(sizes[axis])])]
    pallas_call x2 -> x1, Pallas kernels: 10.2 us -> 4.62 us  [finish(): pl.pallas_call(functools.partial(finish_kernel, sum(groups), groups, len(...]
    dynamic_update_slice x3 -> x0, other arithmetic: 2.88 us -> none  [local(): result = lax.dynamic_update_slice(result, piece, (low, 0))]
    unnamed x23 -> x29, local copies, waits for them, and re-layouts: 4 us -> 1.43 us
    add x1 -> x0, other arithmetic: 2.55 us -> none  [local(): lead = lead + part]
    ppermute x7 -> x23, waiting for transfers between devices: 46.7 us -> 44.5 us  [swap(): return lax.ppermute(x, axis, [(i, i ^ bit) for i in range(sizes[axis])])]
  transfers between devices with their start and end apart: 13 -> 29, of which waited for: 6 -> 13; matrix products, arithmetic and copies ran while one was open for 8% -> 3% of each run, Pallas kernels for 14% -> 23%
where the time goes in v1:
time: 139 us; the launch traced here: 138 us
  waiting for transfers between devices  66.2 us (48%)
  Pallas kernels  41.6 us (30%)
  starting transfers between devices  25.3 us (18%)
  other arithmetic  3.54 us (3%)
  local copies, waits for them, and re-layouts  1.43 us (1%)
    ppermute x23, waiting for transfers between devices, swap(): return lax.ppermute(x, axis, [(i, i ^ bit) for i in range(sizes[axis])])  44.5 us
    ppermute x6, waiting for transfers between devices, pass_states(): received[stage].append(lax.ppermute(sent, ('section', 'dp'), pairs))  21.7 us
    ppermute x23, starting transfers between devices, swap(): return lax.ppermute(x, axis, [(i, i ^ bit) for i in range(sizes[axis])])  16.6 us
    pallas_call x3, Pallas kernels, gather_sum(): pl.pallas_call(functools.partial(gather_kernel, bits, n_rows, n_sources),...  15 us
    ppermute x6, starting transfers between devices, pass_states(): received[stage].append(lax.ppermute(sent, ('section', 'dp'), pairs))  8.75 us
    pallas_call x1, Pallas kernels, chip_sum(): pl.pallas_call(functools.partial(chip_kernel, parts), grid_spec=pltpu.Pre...  6.5 us
    pallas_call x1, Pallas kernels, local(): pl.pallas_call(functools.partial(intra_kernel, heads), in_specs=[SMEM_SPE...  4.96 us
    pallas_call x1, Pallas kernels, finish(): pl.pallas_call(functools.partial(finish_kernel, sum(groups), groups, len(...  4.62 us
  transfers between devices with their start and end apart: 29, of which 13 were waited for; matrix products, arithmetic and copies ran while one was open for 3% of the time, Pallas kernels for 23%

profile of v1, /device:TPU:0, one launch (start us, length us, event | category | flops | bytes accessed | tf_op | source)
XLA Modules:
  0.0 138.3 jit_solution(4778378181728667170)
XLA Ops:
  0.0 4.4 %shard_map.121 = f32[640,1280]{1,0:T(8,128)} custom-call(s32[1]{0:T(128)} %bitcast.5.block_ref, bf16[640,5120]{1,0:T(8,128)(2,1)} %other_in.1), custom_call_target="tpu_custom_call" | custom-call | tf_op jit(solution)/shard_map/pallas_call | solution.py:183
  4.4 0.5 collective-permute-start.6
  4.9 3.8 %shard_map.118 = (f32[3,128,128]{2,1,0:T(8,128)}, f32[2,128,128]{2,1,0:T(8,128)}, f32[3,1,128]{2,1,0:T(1,128)}, f32[2,1,128]{2,1,0:T(1,128)}, f32[8,512]{1,0:T(8...) custom-call(s32[1]{0:T(128)} %bitcast.2.index_ref, s32[5]{0:T(128)} %decay_ref.1, f32[5,512]{1,0:T(8,128)} %bitcast.13, ...), custom_call_target="tpu_custom_call" | custom-call | tf_op jit(solution)/shard_map/pallas_call | solution.py:389
  8.7 2.6 %collective-permute-start.1 = (f32[2,128,128]{2,1,0:T(8,128)}, f32[2,128,128]{2,1,0:T(8,128)S(1)}, u32[]{:S(2)}, u32[]{:S(2)}) collective-permute-start(f32[2,128,128]{2,1,0:T(8,128)} %get-tuple-element.29), channel_id=1, source_target_pairs={{0,8},{1,9},{8,0},{9,1},{16,24},{17,25},{24,16},{25,17},{2,10},{3,... | collective-permute-start | bytes 393224 | tf_op jit(solution)/shard_map/ppermute | solution.py:340
  11.3 4.4 %collective-permute-done.1.rest_1_ = f32[2,128,128]{2,1,0:T(8,128)S(1)} collective-permute-done((f32[2,128,128]{2,1,0:T(8,128)}, f32[2,128,128]{2,1,0:T(8,128)S(1)}, u32[]{:S(2)}, u32[]{:S(2)}) %collective-permute-start.1) | collective-permute-done | bytes 131104 | tf_op jit(solution)/shard_map/ppermute | solution.py:340
  15.6 0.6 copy-done.9
  16.3 1.6 %multiply_add_fusion.3 = f32[2,128,128]{2,1,0:T(8,128)} fusion(f32[2,128,128]{2,1,0:T(8,128)} %get-tuple-element.29, f32[2,128,128]{2,1,0:T(8,128)S(1)} %collective-permute-done.1.rest_1_, f32[2,128]{1,0:T(2,128)} %bitcast.14), kind=kLoop, calls=%fused_computation.3 | loop fusion | flops 65536 | bytes 394240 | tf_op jit(solution)/shard_map/add | solution.py:334
  17.9 1.7 %collective-permute-start.3 = (f32[2,128,128]{2,1,0:T(8,128)}, f32[2,128,128]{2,1,0:T(8,128)}, u32[]{:S(2)}, u32[]{:S(2)}) collective-permute-start(f32[2,128,128]{2,1,0:T(8,128)} %multiply_add_fusion.3), channel_id=1, source_target_pairs={{0,1},{1,0},{8,16},{9,17},{16,8},{17,9},{24,25},{25,24},{2,3},{3,2... | collective-permute-start | bytes 393224 | tf_op jit(solution)/shard_map/ppermute | solution.py:340
  19.5 1.7 %collective-permute-start = (f32[3,128,128]{2,1,0:T(8,128)}, f32[3,128,128]{2,1,0:T(8,128)}, u32[]{:S(2)}, u32[]{:S(2)}) collective-permute-start(f32[3,128,128]{2,1,0:T(8,128)} %get-tuple-element.28), channel_id=1, source_target_pairs={{0,8},{1,9},{8,0},{9,1},{16,24},{17,25},{24,16},{25,17},{2,10},{3,... | collective-permute-start | bytes 589832 | tf_op jit(solution)/shard_map/ppermute | solution.py:340
  21.2 2.4 %shard_map.123 = (f32[80,1280]{1,0:T(8,128)}, f32[80,1280]{1,0:T(8,128)}, f32[80,1280]{1,0:T(8,128)}, f32[80,1280]{1,0:T(8,128)}) custom-call(s32[1]{0:T(128)} %bitcast.row_ref.quarter_ref, s32[1]{0:T(128)} %bitcast.6.block_ref, s32[1]{0:T(128)} %bitcast.7.other_ref, bf16[640,5120]{1,0:T(8,128)(2,1)} %other_in.1, bf16[640,5120]{1,0:T(8,128)(2,1)} %other_in.1), custom_call_target="tpu_custom_call" | custom-call | tf_op jit(solution)/shard_map/pallas_call | solution.py:162
  23.5 1.5 %collective-permute-start.11 = (f32[80,1280]{1,0:T(8,128)}, f32[80,1280]{1,0:T(8,128)}, u32[]{:S(2)}, u32[]{:S(2)}) collective-permute-start(f32[80,1280]{1,0:T(8,128)} %get-tuple-element.36), channel_id=1, source_target_pairs={{0,4},{2,6},{4,0},{6,2},{1,5},{3,7},{5,1},{7,3},{8,12},{10,14},{12... | collective-permute-start | bytes 1228808 | tf_op jit(solution)/shard_map/ppermute | solution.py:373
  25.1 0.5 collective-permute-start.12
  25.7 1.0 multiply_add_fusion.2
  26.7 1.0 collective-permute-start.5
  27.7 0.9 multiply_add_fusion.1
  28.6 3.8 %collective-permute-done.5.rest_5_ = f32[2,128,128]{2,1,0:T(8,128)S(1)} collective-permute-done((f32[2,128,128]{2,1,0:T(8,128)S(1)}, f32[2,128,128]{2,1,0:T(8,128)S(1)}, u32[]{:S(2)}, u32[]{:S(2)}) %collective-permute-start.5) | collective-permute-done | bytes 131104 | tf_op jit(solution)/shard_map/ppermute | solution.py:340
  32.5 1.5 %collective-permute-start.2 = (f32[3,128,128]{2,1,0:T(8,128)S(1)}, f32[3,128,128]{2,1,0:T(8,128)S(1)}, u32[]{:S(2)}, u32[]{:S(2)}) collective-permute-start(f32[3,128,128]{2,1,0:T(8,128)S(1)} %multiply_add_fusion.1), channel_id=1, source_target_pairs={{0,1},{1,0},{8,16},{9,17},{16,8},{17,9},{24,25},{25,24},{2,3},{3,2... | collective-permute-start | bytes 589832 | tf_op jit(solution)/shard_map/ppermute | solution.py:340
  34.0 6.2 %collective-permute-done.2.rest_2_ = f32[3,128,128]{2,1,0:T(8,128)S(1)} collective-permute-done((f32[3,128,128]{2,1,0:T(8,128)S(1)}, f32[3,128,128]{2,1,0:T(8,128)S(1)}, u32[]{:S(2)}, u32[]{:S(2)}) %collective-permute-start.2) | collective-permute-done | bytes 196640 | tf_op jit(solution)/shard_map/ppermute | solution.py:340
  40.1 1.6 %collective-permute-start.15 = (f32[80,1280]{1,0:T(8,128)}, f32[80,1280]{1,0:T(8,128)}, u32[]{:S(2)}, u32[]{:S(2)}) collective-permute-start(f32[80,1280]{1,0:T(8,128)} %collective-permute-done.11.refs_3_), channel_id=1, source_target_pairs={{0,1},{1,0},{2,3},{3,2},{4,5},{5,4},{6,7},{7,6},{8,9},{9,8},{10,11... | collective-permute-start | bytes 1228808 | tf_op jit(solution)/shard_map/ppermute | solution.py:373
  41.7 3.3 %collective-permute-done.12.refs_4_ = f32[80,1280]{1,0:T(8,128)} collective-permute-done((f32[80,1280]{1,0:T(8,128)}, f32[80,1280]{1,0:T(8,128)}, u32[]{:S(2)}, u32[]{:S(2)}) %collective-permute-start.12) | collective-permute-done | bytes 409632 | tf_op jit(solution)/shard_map/ppermute | solution.py:373
  45.0 1.5 %collective-permute-start.16 = (f32[80,1280]{1,0:T(8,128)}, f32[80,1280]{1,0:T(8,128)}, u32[]{:S(2)}, u32[]{:S(2)}) collective-permute-start(f32[80,1280]{1,0:T(8,128)} %collective-permute-done.12.refs_4_), channel_id=1, source_target_pairs={{0,1},{1,0},{2,3},{3,2},{4,5},{5,4},{6,7},{7,6},{8,9},{9,8},{10,11... | collective-permute-start | bytes 1228808 | tf_op jit(solution)/shard_map/ppermute | solution.py:373
  46.5 6.3 %collective-permute-done.13.refs_5_ = f32[80,1280]{1,0:T(8,128)} collective-permute-done((f32[80,1280]{1,0:T(8,128)}, f32[80,1280]{1,0:T(8,128)}, u32[]{:S(2)}, u32[]{:S(2)}) %collective-permute-start.13) | collective-permute-done | bytes 409632 | tf_op jit(solution)/shard_map/ppermute | solution.py:373
  52.8 1.5 %collective-permute-start.17 = (f32[80,1280]{1,0:T(8,128)}, f32[80,1280]{1,0:T(8,128)}, u32[]{:S(2)}, u32[]{:S(2)}) collective-permute-start(f32[80,1280]{1,0:T(8,128)} %collective-permute-done.13.refs_5_), channel_id=1, source_target_pairs={{0,1},{1,0},{2,3},{3,2},{4,5},{5,4},{6,7},{7,6},{8,9},{9,8},{10,11... | collective-permute-start | bytes 1228808 | tf_op jit(solution)/shard_map/ppermute | solution.py:373
  54.3 5.4 %collective-permute-done.14.refs_6_ = f32[80,1280]{1,0:T(8,128)} collective-permute-done((f32[80,1280]{1,0:T(8,128)}, f32[80,1280]{1,0:T(8,128)}, u32[]{:S(2)}, u32[]{:S(2)}) %collective-permute-start.14) | collective-permute-done | bytes 409632 | tf_op jit(solution)/shard_map/ppermute | solution.py:373
  59.7 0.4 collective-permute-start.4
  60.1 7.3 %collective-permute-done.4.rest_4_ = f32[3,128,128]{2,1,0:T(8,128)S(1)} collective-permute-done((f32[3,128,128]{2,1,0:T(8,128)S(1)}, f32[3,128,128]{2,1,0:T(8,128)S(1)}, u32[]{:S(2)}, u32[]{:S(2)}) %collective-permute-start.4) | collective-permute-done | bytes 196640 | tf_op jit(solution)/shard_map/ppermute | solution.py:340
  67.4 1.5 %collective-permute-start.18 = (f32[80,1280]{1,0:T(8,128)}, f32[80,1280]{1,0:T(8,128)}, u32[]{:S(2)}, u32[]{:S(2)}) collective-permute-start(f32[80,1280]{1,0:T(8,128)} %collective-permute-done.14.refs_6_), channel_id=1, source_target_pairs={{0,1},{1,0},{2,3},{3,2},{4,5},{5,4},{6,7},{7,6},{8,9},{9,8},{10,11... | collective-permute-start | bytes 1228808 | tf_op jit(solution)/shard_map/ppermute | solution.py:373
  68.9 0.3 collective-permute-start.19
  69.2 5.0 %shard_map.119 = (f32[512,640]{1,0:T(8,128)}, bf16[512,640]{1,0:T(8,128)(2,1)}) custom-call(s32[1]{0:T(128)} %bitcast.2.index_ref, bf16[512,640]{1,0:T(8,128)(2,1)} %q_ref.1, bf16[512,640]{1,0:T(8,128)(2,1)} %k_ref.3, bf16[512,640]{1,0:T(8,128)(2,1)} %v_ref.3, f32[8,512]{1,0:T(8,128)} %get-tuple-element.23.row_ref, f32[512,8]{1,0:T(8,128)} %get-tuple-element.24.column_ref, ...), custom_call_target="tpu_custom_call" | custom-call | flops 671088640 | bytes 3932160 | tf_op jit(solution)/shard_map/pallas_call | solution.py:407
  74.1 1.8 %collective-permute-start.20 = (f32[80,1280]{1,0:T(8,128)}, f32[80,1280]{1,0:T(8,128)}, u32[]{:S(2)}, u32[]{:S(2)}) collective-permute-start(f32[80,1280]{1,0:T(8,128)} %collective-permute-done.12.refs_4_), channel_id=1, source_target_pairs={{0,8},{8,0},{16,24},{24,16},{1,9},{9,1},{17,25},{25,17},{2,10},{10... | collective-permute-start | bytes 1228808 | tf_op jit(solution)/shard_map/ppermute | solution.py:373
  75.9 4.6 %shard_map.120 = (bf16[512,640]{1,0:T(8,128)(2,1)}, f32[256,640]{1,0:T(8,128)}, f32[256,640]{1,0:T(8,128)}) custom-call(s32[1]{0:T(128)} %bitcast.2.index_ref, f32[512,640]{1,0:T(8,128)} %get-tuple-element.25.intra_ref, bf16[512,640]{1,0:T(8,128)(2,1)} %get-tuple-element.26.rot_ref, f32[512,8]{1,0:T(8,128)} %get-tuple-element.27.grown_ref, f32[640]{0:T(1024)} %gain_ref.1, ...), custom_call_target="tpu_custom_call" | custom-call | tf_op jit(solution)/shard_map/pallas_call | solution.py:226
  80.6 0.5 collective-permute-start.21
  81.1 0.4 collective-permute-done.19.refs_11_
  81.5 1.1 collective-permute-start.22
  82.7 7.6 %collective-permute-done.20.refs_12_ = f32[80,1280]{1,0:T(8,128)} collective-permute-done((f32[80,1280]{1,0:T(8,128)}, f32[80,1280]{1,0:T(8,128)}, u32[]{:S(2)}, u32[]{:S(2)}) %collective-permute-start.20) | collective-permute-done | bytes 409632 | tf_op jit(solution)/shard_map/ppermute | solution.py:373
  90.3 8.7 %collective-permute-done.21.refs_13_ = f32[80,1280]{1,0:T(8,128)S(1)} collective-permute-done((f32[80,1280]{1,0:T(8,128)}, f32[80,1280]{1,0:T(8,128)S(1)}, u32[]{:S(2)}, u32[]{:S(2)}) %collective-permute-start.21) | collective-permute-done | bytes 409632 | tf_op jit(solution)/shard_map/ppermute | solution.py:373
  99.0 7.9 %collective-permute-done.22.refs_14_ = f32[80,1280]{1,0:T(8,128)S(1)} collective-permute-done((f32[80,1280]{1,0:T(8,128)}, f32[80,1280]{1,0:T(8,128)S(1)}, u32[]{:S(2)}, u32[]{:S(2)}) %collective-permute-start.22) | collective-permute-done | bytes 409632 | tf_op jit(solution)/shard_map/ppermute | solution.py:373
  106.8 0.7 copy-done.4
  107.6 3.4 %collective-permute-done.9.refs_1_.refs_2_ = f32[256,640]{1,0:T(8,128)} collective-permute-done((f32[256,640]{1,0:T(8,128)}, f32[256,640]{1,0:T(8,128)}, u32[]{:S(2)}, u32[]{:S(2)}) %collective-permute-start.9) | collective-permute-done | bytes 655392 | tf_op jit(solution)/shard_map/ppermute | solution.py:373
  111.1 0.6 collective-permute-start.25
  111.7 1.5 %collective-permute-start.26 = (f32[80,1280]{1,0:T(8,128)}, f32[80,1280]{1,0:T(8,128)}, u32[]{:S(2)}, u32[]{:S(2)}) collective-permute-start(f32[80,1280]{1,0:T(8,128)} %collective-permute-done.20.refs_12_), channel_id=1, source_target_pairs={{0,1},{1,0},{2,3},{3,2},{4,5},{5,4},{6,7},{7,6},{8,9},{9,8},{10,11... | collective-permute-start | bytes 1228808 | tf_op jit(solution)/shard_map/ppermute | solution.py:373
  113.2 0.3 collective-permute-start.27
  113.5 1.8 %collective-permute-start.28 = (f32[80,1280]{1,0:T(8,128)}, f32[80,1280]{1,0:T(8,128)}, u32[]{:S(2)}, u32[]{:S(2)}) collective-permute-start(f32[80,1280]{1,0:T(8,128)} %collective-permute-done.18.refs_10_), channel_id=1, source_target_pairs={{0,8},{8,0},{16,24},{24,16},{1,9},{9,1},{17,25},{25,17},{2,10},{10... | collective-permute-start | bytes 1228808 | tf_op jit(solution)/shard_map/ppermute | solution.py:373
  115.3 6.5 %shard_map.122 = (f32[256,1280]{1,0:T(8,128)}, f32[256,1280]{1,0:T(8,128)}) custom-call(s32[1]{0:T(128)} %bitcast.1.block_ref, bf16[512,640]{1,0:T(8,128)(2,1)} %get-tuple-element.32.kept_ref, bf16[640,5120]{1,0:T(8,128)(2,1)} %other_in.1, f32[640,1280]{1,0:T(8,128)} %copy-done, bf16[512,1280]{1,0:T(8,128)(2,1)} %hidden_ref.1, f32[256,640]{1,0:T(8,128)} %copy-done.7, ...), custom_call_target="tpu_custom_call" | custom-call | tf_op jit(solution)/shard_map/pallas_call | solution.py:251
  121.8 5.1 %shard_map.125.refs_1_ = f32[256,1280]{1,0:T(8,128)} custom-call(s32[1]{0:T(128)} %bitcast.row_ref.quarter_ref, f32[256,1280]{1,0:T(8,128)} %get-tuple-element.40.refs_0_, f32[256,640]{1,0:T(8,128)} %copy-done.1, f32[256,640]{1,0:T(8,128)} %copy-done.2, f32[80,1280]{1,0:T(8,128)} %collective-permute-done.11.refs_3_, ...), custom_call_target="tpu_custom_call" | custom-call | tf_op jit(solution)/shard_map/pallas_call | solution.py:311
  126.9 5.1 %shard_map.124.refs_0_ = f32[256,1280]{1,0:T(8,128)} custom-call(s32[1]{0:T(128)} %bitcast.row_ref.quarter_ref, f32[256,1280]{1,0:T(8,128)} %get-tuple-element.35.refs_0_, f32[256,640]{1,0:T(8,128)} %collective-permute-done.9.refs_1_.refs_2_, f32[256,640]{1,0:T(8,128)} %collective-permute-done.10.refs_2_.refs_3_, ...), custom_call_target="tpu_custom_call" | custom-call | tf_op jit(solution)/shard_map/pallas_call | solution.py:311
  132.0 1.5 %collective-permute-done.28.refs_9_ = f32[80,1280]{1,0:T(8,128)} collective-permute-done((f32[80,1280]{1,0:T(8,128)}, f32[80,1280]{1,0:T(8,128)}, u32[]{:S(2)}, u32[]{:S(2)}) %collective-permute-start.28) | collective-permute-done | bytes 409632 | tf_op jit(solution)/shard_map/ppermute | solution.py:373
  133.5 4.8 %shard_map.126 = bf16[512,1280]{1,0:T(8,128)(2,1)} custom-call(s32[1]{0:T(128)} %bitcast.row_ref.quarter_ref, f32[256,1280]{1,0:T(8,128)} %shard_map.124.refs_0_, f32[256,1280]{1,0:T(8,128)} %shard_map.125.refs_1_, f32[256,640]{1,0:T(8,128)} %collective-permute-done.9.refs_1_.refs_2_, f32[256,640]{1,0:T(8,128)} %collective-permute-done.10.refs_2_.refs_3_, ...), custom_call_target="tpu_custom_call" | custom-call | tf_op jit(solution)/shard_map/pallas_call | solution.py:311
  (52 shorter events, 0.2 us)
Async XLA Ops:
  4.4 109.0 %collective-permute-start.6 = (f32[640,1280]{1,0:T(8,128)}, f32[640,1280]{1,0:T(8,128)S(1)}, u32[]{:S(2)}, u32[]{:S(2)}) collective-permute-start(f32[640,1280]{1,0:T(8,128)} %shard_map.121), channel_id=1, source_target_pairs={{0,2},{2,0},{4,6},{6,4},{1,3},{3,1},{5,7},{7,5},{8,10},{10,8},{12,... | collective-permute-start | bytes 9830408 | tf_op jit(solution)/shard_map/ppermute | solution.py:373
  8.7 6.9 %collective-permute-start.1 = (f32[2,128,128]{2,1,0:T(8,128)}, f32[2,128,128]{2,1,0:T(8,128)S(1)}, u32[]{:S(2)}, u32[]{:S(2)}) collective-permute-start(f32[2,128,128]{2,1,0:T(8,128)} %get-tuple-element.29), channel_id=1, source_target_pairs={{0,8},{1,9},{8,0},{9,1},{16,24},{17,25},{24,16},{25,17},{2,10},{3,... | collective-permute-start | bytes 393224 | tf_op jit(solution)/shard_map/ppermute | solution.py:340
  15.6 0.6 copy-start.9
  17.9 7.7 %collective-permute-start.3 = (f32[2,128,128]{2,1,0:T(8,128)}, f32[2,128,128]{2,1,0:T(8,128)}, u32[]{:S(2)}, u32[]{:S(2)}) collective-permute-start(f32[2,128,128]{2,1,0:T(8,128)} %multiply_add_fusion.3), channel_id=1, source_target_pairs={{0,1},{1,0},{8,16},{9,17},{16,8},{17,9},{24,25},{25,24},{2,3},{3,2... | collective-permute-start | bytes 393224 | tf_op jit(solution)/shard_map/ppermute | solution.py:340
  19.5 7.1 %collective-permute-start = (f32[3,128,128]{2,1,0:T(8,128)}, f32[3,128,128]{2,1,0:T(8,128)}, u32[]{:S(2)}, u32[]{:S(2)}) collective-permute-start(f32[3,128,128]{2,1,0:T(8,128)} %get-tuple-element.28), channel_id=1, source_target_pairs={{0,8},{1,9},{8,0},{9,1},{16,24},{17,25},{24,16},{25,17},{2,10},{3,... | collective-permute-start | bytes 589832 | tf_op jit(solution)/shard_map/ppermute | solution.py:340
  21.2 4.4 %copy-start.13 = (f32[3,1,128]{2,1,0:T(1,128)S(1)}, f32[3,1,128]{2,1,0:T(1,128)}, u32[]{:S(2)}) copy-start(f32[3,1,128]{2,1,0:T(1,128)} %get-tuple-element.30) | copy-start | bytes 4612
  21.2 4.5 %copy-start.12 = (f32[2,1,128]{2,1,0:T(1,128)S(1)}, f32[2,1,128]{2,1,0:T(1,128)}, u32[]{:S(2)}) copy-start(f32[2,1,128]{2,1,0:T(1,128)} %get-tuple-element.31) | copy-start | bytes 3076
  21.2 6.5 %copy-start.5 = (f32[3,128,128]{2,1,0:T(8,128)S(1)}, f32[3,128,128]{2,1,0:T(8,128)}, u32[]{:S(2)}) copy-start(f32[3,128,128]{2,1,0:T(8,128)} %get-tuple-element.28) | copy-start | bytes 589828
  23.5 16.6 %collective-permute-start.11 = (f32[80,1280]{1,0:T(8,128)}, f32[80,1280]{1,0:T(8,128)}, u32[]{:S(2)}, u32[]{:S(2)}) collective-permute-start(f32[80,1280]{1,0:T(8,128)} %get-tuple-element.36), channel_id=1, source_target_pairs={{0,4},{2,6},{4,0},{6,2},{1,5},{3,7},{5,1},{7,3},{8,12},{10,14},{12... | collective-permute-start | bytes 1228808 | tf_op jit(solution)/shard_map/ppermute | solution.py:373
  25.1 19.9 %collective-permute-start.12 = (f32[80,1280]{1,0:T(8,128)}, f32[80,1280]{1,0:T(8,128)}, u32[]{:S(2)}, u32[]{:S(2)}) collective-permute-start(f32[80,1280]{1,0:T(8,128)} %get-tuple-element.37), channel_id=1, source_target_pairs={{0,4},{2,6},{4,0},{6,2},{1,5},{3,7},{5,1},{7,3},{8,12},{10,14},{12... | collective-permute-start | bytes 1228808 | tf_op jit(solution)/shard_map/ppermute | solution.py:373
  25.6 27.2 %collective-permute-start.13 = (f32[80,1280]{1,0:T(8,128)}, f32[80,1280]{1,0:T(8,128)}, u32[]{:S(2)}, u32[]{:S(2)}) collective-permute-start(f32[80,1280]{1,0:T(8,128)} %get-tuple-element.38), channel_id=1, source_target_pairs={{0,6},{2,4},{4,2},{6,0},{1,7},{3,5},{5,3},{7,1},{8,14},{10,12},{12... | collective-permute-start | bytes 1228808 | tf_op jit(solution)/shard_map/ppermute | solution.py:373
  26.7 5.8 %collective-permute-start.5 = (f32[2,128,128]{2,1,0:T(8,128)S(1)}, f32[2,128,128]{2,1,0:T(8,128)S(1)}, u32[]{:S(2)}, u32[]{:S(2)}) collective-permute-start(f32[2,128,128]{2,1,0:T(8,128)S(1)} %multiply_add_fusion.2), channel_id=1, source_target_pairs={{0,8},{1,9},{8,0},{9,1},{16,24},{17,25},{24,16},{25,17},{2,10},{3,... | collective-permute-start | bytes 393224 | tf_op jit(solution)/shard_map/ppermute | solution.py:340
  32.5 34.9 %copy-start.11 = (f32[2,128,128]{2,1,0:T(8,128)}, f32[2,128,128]{2,1,0:T(8,128)S(1)}, u32[]{:S(2)}) copy-start(f32[2,128,128]{2,1,0:T(8,128)S(1)} %collective-permute-done.5.rest_5_) | copy-start | bytes 393220
  32.5 7.7 %collective-permute-start.2 = (f32[3,128,128]{2,1,0:T(8,128)S(1)}, f32[3,128,128]{2,1,0:T(8,128)S(1)}, u32[]{:S(2)}, u32[]{:S(2)}) collective-permute-start(f32[3,128,128]{2,1,0:T(8,128)S(1)} %multiply_add_fusion.1), channel_id=1, source_target_pairs={{0,1},{1,0},{8,16},{9,17},{16,8},{17,9},{24,25},{25,24},{2,3},{3,2... | collective-permute-start | bytes 589832 | tf_op jit(solution)/shard_map/ppermute | solution.py:340
  40.1 14.2 %copy-start.6 = (f32[3,128,128]{2,1,0:T(8,128)}, f32[3,128,128]{2,1,0:T(8,128)S(1)}, u32[]{:S(2)}) copy-start(f32[3,128,128]{2,1,0:T(8,128)S(1)} %collective-permute-done.2.rest_2_) | copy-start | bytes 589828
  40.1 19.6 %collective-permute-start.14 = (f32[80,1280]{1,0:T(8,128)}, f32[80,1280]{1,0:T(8,128)}, u32[]{:S(2)}, u32[]{:S(2)}) collective-permute-start(f32[80,1280]{1,0:T(8,128)} %get-tuple-element.39), channel_id=1, source_target_pairs={{0,6},{2,4},{4,2},{6,0},{1,7},{3,5},{5,3},{7,1},{8,14},{10,12},{12... | collective-permute-start | bytes 1228808 | tf_op jit(solution)/shard_map/ppermute | solution.py:373
  40.1 28.7 %collective-permute-start.15 = (f32[80,1280]{1,0:T(8,128)}, f32[80,1280]{1,0:T(8,128)}, u32[]{:S(2)}, u32[]{:S(2)}) collective-permute-start(f32[80,1280]{1,0:T(8,128)} %collective-permute-done.11.refs_3_), channel_id=1, source_target_pairs={{0,1},{1,0},{2,3},{3,2},{4,5},{5,4},{6,7},{7,6},{8,9},{9,8},{10,11... | collective-permute-start | bytes 1228808 | tf_op jit(solution)/shard_map/ppermute | solution.py:373
  45.0 29.1 %collective-permute-start.16 = (f32[80,1280]{1,0:T(8,128)}, f32[80,1280]{1,0:T(8,128)}, u32[]{:S(2)}, u32[]{:S(2)}) collective-permute-start(f32[80,1280]{1,0:T(8,128)} %collective-permute-done.12.refs_4_), channel_id=1, source_target_pairs={{0,1},{1,0},{2,3},{3,2},{4,5},{5,4},{6,7},{7,6},{8,9},{9,8},{10,11... | collective-permute-start | bytes 1228808 | tf_op jit(solution)/shard_map/ppermute | solution.py:373
  52.8 27.8 %collective-permute-start.17 = (f32[80,1280]{1,0:T(8,128)}, f32[80,1280]{1,0:T(8,128)}, u32[]{:S(2)}, u32[]{:S(2)}) collective-permute-start(f32[80,1280]{1,0:T(8,128)} %collective-permute-done.13.refs_5_), channel_id=1, source_target_pairs={{0,1},{1,0},{2,3},{3,2},{4,5},{5,4},{6,7},{7,6},{8,9},{9,8},{10,11... | collective-permute-start | bytes 1228808 | tf_op jit(solution)/shard_map/ppermute | solution.py:373
  59.7 7.7 %collective-permute-start.4 = (f32[3,128,128]{2,1,0:T(8,128)S(1)}, f32[3,128,128]{2,1,0:T(8,128)S(1)}, u32[]{:S(2)}, u32[]{:S(2)}) collective-permute-start(f32[3,128,128]{2,1,0:T(8,128)S(1)} %multiply_add_fusion), channel_id=1, source_target_pairs={{0,8},{1,9},{8,0},{9,1},{16,24},{17,25},{24,16},{25,17},{2,10},{3,... | collective-permute-start | bytes 589832 | tf_op jit(solution)/shard_map/ppermute | solution.py:340
  67.4 6.8 %copy-start.10 = (f32[3,128,128]{2,1,0:T(8,128)}, f32[3,128,128]{2,1,0:T(8,128)S(1)}, u32[]{:S(2)}) copy-start(f32[3,128,128]{2,1,0:T(8,128)S(1)} %collective-permute-done.4.rest_4_) | copy-start | bytes 589828
  67.4 13.2 %collective-permute-start.18 = (f32[80,1280]{1,0:T(8,128)}, f32[80,1280]{1,0:T(8,128)}, u32[]{:S(2)}, u32[]{:S(2)}) collective-permute-start(f32[80,1280]{1,0:T(8,128)} %collective-permute-done.14.refs_6_), channel_id=1, source_target_pairs={{0,1},{1,0},{2,3},{3,2},{4,5},{5,4},{6,7},{7,6},{8,9},{9,8},{10,11... | collective-permute-start | bytes 1228808 | tf_op jit(solution)/shard_map/ppermute | solution.py:373
  68.9 12.7 %collective-permute-start.19 = (f32[80,1280]{1,0:T(8,128)}, f32[80,1280]{1,0:T(8,128)}, u32[]{:S(2)}, u32[]{:S(2)}) collective-permute-start(f32[80,1280]{1,0:T(8,128)} %collective-permute-done.11.refs_3_), channel_id=1, source_target_pairs={{0,8},{8,0},{16,24},{24,16},{1,9},{9,1},{17,25},{25,17},{2,10},{10... | collective-permute-start | bytes 1228808 | tf_op jit(solution)/shard_map/ppermute | solution.py:373
  74.1 16.2 %collective-permute-start.20 = (f32[80,1280]{1,0:T(8,128)}, f32[80,1280]{1,0:T(8,128)}, u32[]{:S(2)}, u32[]{:S(2)}) collective-permute-start(f32[80,1280]{1,0:T(8,128)} %collective-permute-done.12.refs_4_), channel_id=1, source_target_pairs={{0,8},{8,0},{16,24},{24,16},{1,9},{9,1},{17,25},{25,17},{2,10},{10... | collective-permute-start | bytes 1228808 | tf_op jit(solution)/shard_map/ppermute | solution.py:373
  80.6 27.0 %collective-permute-start.23 = (f32[256,640]{1,0:T(8,128)}, f32[256,640]{1,0:T(8,128)S(1)}, u32[]{:S(2)}, u32[]{:S(2)}) collective-permute-start(f32[256,640]{1,0:T(8,128)} %get-tuple-element.34), channel_id=1, source_target_pairs={{0,4},{2,6},{4,0},{6,2},{1,5},{3,7},{5,1},{7,3},{8,12},{10,14},{12... | collective-permute-start | bytes 1966088 | tf_op jit(solution)/shard_map/ppermute | solution.py:373
  80.6 18.4 %collective-permute-start.21 = (f32[80,1280]{1,0:T(8,128)}, f32[80,1280]{1,0:T(8,128)S(1)}, u32[]{:S(2)}, u32[]{:S(2)}) collective-permute-start(f32[80,1280]{1,0:T(8,128)} %collective-permute-done.13.refs_5_), channel_id=1, source_target_pairs={{0,8},{8,0},{16,24},{24,16},{1,9},{9,1},{17,25},{25,17},{2,10},{10... | collective-permute-start | bytes 1228808 | tf_op jit(solution)/shard_map/ppermute | solution.py:373
  81.5 25.3 %collective-permute-start.22 = (f32[80,1280]{1,0:T(8,128)}, f32[80,1280]{1,0:T(8,128)S(1)}, u32[]{:S(2)}, u32[]{:S(2)}) collective-permute-start(f32[80,1280]{1,0:T(8,128)} %collective-permute-done.14.refs_6_), channel_id=1, source_target_pairs={{0,8},{8,0},{16,24},{24,16},{1,9},{9,1},{17,25},{25,17},{2,10},{10... | collective-permute-start | bytes 1228808 | tf_op jit(solution)/shard_map/ppermute | solution.py:373
  90.3 20.8 %collective-permute-start.9 = (f32[256,640]{1,0:T(8,128)}, f32[256,640]{1,0:T(8,128)}, u32[]{:S(2)}, u32[]{:S(2)}) collective-permute-start(f32[256,640]{1,0:T(8,128)} %get-tuple-element.33), channel_id=1, source_target_pairs={{0,4},{2,6},{4,0},{6,2},{1,5},{3,7},{5,1},{7,3},{8,12},{10,14},{12... | collective-permute-start | bytes 1966088 | tf_op jit(solution)/shard_map/ppermute | solution.py:373
  99.0 7.9 %copy-start.3 = (f32[80,1280]{1,0:T(8,128)}, f32[80,1280]{1,0:T(8,128)S(1)}, u32[]{:S(2)}) copy-start(f32[80,1280]{1,0:T(8,128)S(1)} %collective-permute-done.21.refs_13_) | copy-start | bytes 1228804
  99.0 12.1 %collective-permute-start.7 = (f32[256,640]{1,0:T(8,128)}, f32[256,640]{1,0:T(8,128)S(1)}, u32[]{:S(2)}, u32[]{:S(2)}) collective-permute-start(f32[256,640]{1,0:T(8,128)} %get-tuple-element.33), channel_id=1, source_target_pairs={{0,2},{2,0},{4,6},{6,4},{1,3},{3,1},{5,7},{7,5},{8,10},{10,8},{12,... | collective-permute-start | bytes 1966088 | tf_op jit(solution)/shard_map/ppermute | solution.py:373
  106.8 0.8 copy-start.4
  106.8 4.8 %collective-permute-start.8 = (f32[256,640]{1,0:T(8,128)}, f32[256,640]{1,0:T(8,128)S(1)}, u32[]{:S(2)}, u32[]{:S(2)}) collective-permute-start(f32[256,640]{1,0:T(8,128)} %get-tuple-element.34), channel_id=1, source_target_pairs={{0,2},{2,0},{4,6},{6,4},{1,3},{3,1},{5,7},{7,5},{8,10},{10,8},{12,... | collective-permute-start | bytes 1966088 | tf_op jit(solution)/shard_map/ppermute | solution.py:373
  107.6 5.9 %copy-start.1 = (f32[256,640]{1,0:T(8,128)}, f32[256,640]{1,0:T(8,128)S(1)}, u32[]{:S(2)}) copy-start(f32[256,640]{1,0:T(8,128)S(1)} %collective-permute-done.23.refs_1_.refs_4_) | copy-start | bytes 1966084
  107.6 5.6 %collective-permute-start.24 = (f32[256,640]{1,0:T(8,128)S(1)}, f32[256,640]{1,0:T(8,128)S(1)}, u32[]{:S(2)}, u32[]{:S(2)}) collective-permute-start(f32[256,640]{1,0:T(8,128)S(1)} %collective-permute-done.23.refs_1_.refs_4_), channel_id=1, source_target_pairs={{0,2},{2,0},{4,6},{6,4},{1,3},{3,1},{5,7},{7,5},{8,10},{10,8},{12,... | collective-permute-start | bytes 1966088 | tf_op jit(solution)/shard_map/ppermute | solution.py:373
  111.0 15.8 %collective-permute-start.10 = (f32[256,640]{1,0:T(8,128)}, f32[256,640]{1,0:T(8,128)}, u32[]{:S(2)}, u32[]{:S(2)}) collective-permute-start(f32[256,640]{1,0:T(8,128)} %collective-permute-done.9.refs_1_.refs_2_), channel_id=1, source_target_pairs={{0,2},{2,0},{4,6},{6,4},{1,3},{3,1},{5,7},{7,5},{8,10},{10,8},{12,... | collective-permute-start | bytes 1966088 | tf_op jit(solution)/shard_map/ppermute | solution.py:373
  111.1 4.2 %copy-start.7 = (f32[256,640]{1,0:T(8,128)}, f32[256,640]{1,0:T(8,128)S(1)}, u32[]{:S(2)}) copy-start(f32[256,640]{1,0:T(8,128)S(1)} %collective-permute-done.7.rest_0_) | copy-start | bytes 1966084
  111.1 21.0 %collective-permute-start.25 = (f32[80,1280]{1,0:T(8,128)}, f32[80,1280]{1,0:T(8,128)}, u32[]{:S(2)}, u32[]{:S(2)}) collective-permute-start(f32[80,1280]{1,0:T(8,128)} %collective-permute-done.19.refs_11_), channel_id=1, source_target_pairs={{0,1},{1,0},{2,3},{3,2},{4,5},{5,4},{6,7},{7,6},{8,9},{9,8},{10,11... | collective-permute-start | bytes 1228808 | tf_op jit(solution)/shard_map/ppermute | solution.py:373
  111.7 3.6 %copy-start.8 = (f32[256,640]{1,0:T(8,128)}, f32[256,640]{1,0:T(8,128)S(1)}, u32[]{:S(2)}) copy-start(f32[256,640]{1,0:T(8,128)S(1)} %collective-permute-done.8.rest_1_) | copy-start | bytes 1966084
  111.7 20.4 %collective-permute-start.26 = (f32[80,1280]{1,0:T(8,128)}, f32[80,1280]{1,0:T(8,128)}, u32[]{:S(2)}, u32[]{:S(2)}) collective-permute-start(f32[80,1280]{1,0:T(8,128)} %collective-permute-done.20.refs_12_), channel_id=1, source_target_pairs={{0,1},{1,0},{2,3},{3,2},{4,5},{5,4},{6,7},{7,6},{8,9},{9,8},{10,11... | collective-permute-start | bytes 1228808 | tf_op jit(solution)/shard_map/ppermute | solution.py:373
  113.2 2.1 %copy-start.2 = (f32[256,640]{1,0:T(8,128)}, f32[256,640]{1,0:T(8,128)S(1)}, u32[]{:S(2)}) copy-start(f32[256,640]{1,0:T(8,128)S(1)} %collective-permute-done.24.refs_2_.refs_5_) | copy-start | bytes 1966084
  113.2 18.9 %collective-permute-start.27 = (f32[80,1280]{1,0:T(8,128)}, f32[80,1280]{1,0:T(8,128)}, u32[]{:S(2)}, u32[]{:S(2)}) collective-permute-start(f32[80,1280]{1,0:T(8,128)} %collective-permute-done.17.refs_9_), channel_id=1, source_target_pairs={{0,8},{8,0},{16,24},{24,16},{1,9},{9,1},{17,25},{25,17},{2,10},{10... | collective-permute-start | bytes 1228808 | tf_op jit(solution)/shard_map/ppermute | solution.py:373
  113.5 1.8 %copy-start = (f32[640,1280]{1,0:T(8,128)}, f32[640,1280]{1,0:T(8,128)S(1)}, u32[]{:S(2)}) copy-start(f32[640,1280]{1,0:T(8,128)S(1)} %collective-permute-done.6.wide_ref) | copy-start | bytes 9830404
  113.5 20.0 %collective-permute-start.28 = (f32[80,1280]{1,0:T(8,128)}, f32[80,1280]{1,0:T(8,128)}, u32[]{:S(2)}, u32[]{:S(2)}) collective-permute-start(f32[80,1280]{1,0:T(8,128)} %collective-permute-done.18.refs_10_), channel_id=1, source_target_pairs={{0,8},{8,0},{16,24},{24,16},{1,9},{9,1},{17,25},{25,17},{2,10},{10... | collective-permute-start | bytes 1228808 | tf_op jit(solution)/shard_map/ppermute | solution.py:373
